TPU v7x, 512 devices: a whole 4x4x16 slice. The times are simulated.
512 devices in a mesh: seq: 64 (over z_lo, y, core), dp: 8 (over z_hi, x).
Axes of the slice: x: 4, y: 4, z: 16 (z_hi: 2, z_lo: 8; z = z_hi * 8 + z_lo), core: 2. Of those that a mesh axis runs over, the one named last changes fastest.
Arguments:
- q_raw: bfloat16 [8, 16384, 1024], P('dp', 'seq'), may hold values from -400 to 400
- k_raw: bfloat16 [8, 16384, 512], P('dp', 'seq'), may hold values from -400 to 400
- values: bfloat16 [8, 16384, 512], P('dp', 'seq'), may hold values from -6 to 6
- grad_out: bfloat16 [8, 16384, 1024], P('dp', 'seq'), may hold values from -80 to 80
- q_gain: float32 [256], replicated, may hold values from 0.5 to 7
- k_gain: float32 [256], replicated, may hold values from 0.5 to 7
Outputs:
- grad_q_raw: bfloat16 [8, 16384, 1024], P('dp', 'seq')
- grad_k_raw: bfloat16 [8, 16384, 512], P('dp', 'seq')
- grad_values: bfloat16 [8, 16384, 512], P('dp', 'seq')
- grad_q_gain: float32 [256], replicated
- grad_k_gain: float32 [256], replicated
All inputs are finite; a program needn't handle non-finite values.
Results may differ from a plain program's by a relative error of at most 0.029.
The roundings to bfloat16 on the way count: a program that leaves them out, or rounds other values in their place, can miss the bound.
Values may be sent and summed in bfloat16 or wider, within the bound.
A program may use at most 128 MiB of HBM per device.

v0:
```python
import jax
import jax.numpy as jnp
from jax import lax
from jax.sharding import PartitionSpec as P

WINDOW = 1024


EPS = 1e-06
ROPE_BASE = 10000.0
MASKED = -1e30


def from_behind(array, axis, by):
    count = lax.axis_size(axis)
    pairs = [(i, i + by) for i in range(count) if 0 <= i + by < count]
    return lax.ppermute(array, axis, pairs)


def rope_tables(positions, head_size):
    half_size = head_size // 2
    freqs = jnp.power(ROPE_BASE, -(2.0 * jnp.arange(half_size, dtype=jnp.float32)) / head_size)
    angles = positions.astype(jnp.float32)[:, None] * freqs[None, :]
    return (jnp.cos(angles), jnp.sin(angles))


def norm_rope(raw_in, gain_in, cosine, sine, head_count):
    head_size = gain_in.shape[0]
    row_count = raw_in.shape[0]
    inputs = raw_in.reshape(row_count, head_count, head_size)
    inverse = lax.rsqrt(jnp.mean(inputs * inputs, axis=-1, keepdims=True) + EPS)
    scaled = inputs * inverse * gain_in
    half_size = head_size // 2
    lower = scaled[..., :half_size]
    upper = scaled[..., half_size:]
    cos_rows = cosine[:, None, :]
    sin_rows = sine[:, None, :]
    turned = jnp.concatenate(
        [lower * cos_rows - upper * sin_rows, upper * cos_rows + lower * sin_rows], axis=-1
    )
    return turned.reshape(row_count, head_count * head_size)


def local(q_raw, k_raw, values, grad_out, q_gain, k_gain):
    q_local = q_raw[0]
    k_local = k_raw[0]
    v_local = values[0]
    do_local = grad_out[0]
    rows_here = q_local.shape[0]
    head_size = q_gain.shape[0]
    query_heads = q_local.shape[1] // head_size
    pair_heads = k_local.shape[1] // head_size
    group_size = query_heads // pair_heads
    reach_dev = WINDOW // rows_here
    key_span = WINDOW + rows_here
    score_scale = head_size ** (-0.5)
    first_pos = lax.axis_index("seq") * rows_here
    positions = first_pos + jnp.arange(rows_here, dtype=jnp.int32)
    cosine, sine = rope_tables(positions, head_size)
    q_rot32, q_back = jax.vjp(
        lambda raw_in, gain_in: norm_rope(raw_in, gain_in, cosine, sine, query_heads),
        q_local.astype(jnp.float32),
        q_gain,
    )
    k_rot32, k_back = jax.vjp(
        lambda raw_in, gain_in: norm_rope(raw_in, gain_in, cosine, sine, pair_heads),
        k_local.astype(jnp.float32),
        k_gain,
    )
    q_rot = q_rot32.astype(jnp.bfloat16)
    k_rot = k_rot32.astype(jnp.bfloat16)
    halo_k = []
    halo_v = []
    for offset in range(reach_dev, 0, -1):
        received = from_behind((k_rot, v_local), "seq", offset)
        halo_k.append(received[0])
        halo_v.append(received[1])
    key_rows = jnp.concatenate(halo_k + [k_rot], axis=0)
    value_rows = jnp.concatenate(halo_v + [v_local], axis=0)
    q_heads = q_rot.reshape(rows_here, pair_heads, group_size, head_size)
    k_heads = key_rows.reshape(key_span, pair_heads, head_size)
    v_heads = value_rows.reshape(key_span, pair_heads, head_size)
    do_heads = do_local.reshape(rows_here, pair_heads, group_size, head_size)
    query_idx = jnp.arange(rows_here, dtype=jnp.int32)[:, None]
    key_idx = jnp.arange(key_span, dtype=jnp.int32)[None, :]
    distance = query_idx + WINDOW - key_idx
    visible = (distance >= 0) & (distance < WINDOW) & (key_idx >= WINDOW - first_pos)
    scores = (
        jnp.einsum("tkgd,skd->kgts", q_heads, k_heads, preferred_element_type=jnp.float32)
        * score_scale
    )
    scores = jnp.where(visible, scores, MASKED)
    row_top = jnp.max(scores, axis=-1, keepdims=True)
    row_total = jnp.log(jnp.sum(jnp.exp(scores - row_top), axis=-1, keepdims=True)) + row_top
    weights = jnp.exp(scores - row_total)
    weights_b = weights.astype(jnp.bfloat16)
    dweights = jnp.einsum("tkgd,skd->kgts", do_heads, v_heads, preferred_element_type=jnp.float32)
    row_delta = jnp.sum(weights * dweights, axis=-1, keepdims=True)
    dscores = (weights * (dweights - row_delta) * score_scale).astype(jnp.bfloat16)
    dq_rot = jnp.einsum(
        "kgts,skd->tkgd", dscores, k_heads, preferred_element_type=jnp.float32
    ).reshape(rows_here, query_heads * head_size)
    dk_all = jnp.einsum("kgts,tkgd->skd", dscores, q_heads, preferred_element_type=jnp.float32)
    dv_all = jnp.einsum("kgts,tkgd->skd", weights_b, do_heads, preferred_element_type=jnp.float32)
    dk_own = dk_all[WINDOW:]
    dv_own = dv_all[WINDOW:]
    for offset in range(1, reach_dev + 1):
        low_row = (reach_dev - offset) * rows_here
        sent_k = dk_all[low_row : low_row + rows_here].astype(jnp.bfloat16)
        sent_v = dv_all[low_row : low_row + rows_here].astype(jnp.bfloat16)
        received = from_behind((sent_k, sent_v), "seq", -offset)
        dk_own = dk_own + received[0].astype(jnp.float32)
        dv_own = dv_own + received[1].astype(jnp.float32)
    dk_rot = dk_own.reshape(rows_here, pair_heads * head_size)
    grad_q_local, gain_q_local = q_back(dq_rot)
    grad_k_local, gain_k_local = k_back(dk_rot)
    gain_q_all, gain_k_all = lax.psum((gain_q_local, gain_k_local), ("seq", "dp"))
    grad_v_local = dv_own.reshape(rows_here, pair_heads * head_size).astype(jnp.bfloat16)
    return (
        grad_q_local.astype(jnp.bfloat16)[None],
        grad_k_local.astype(jnp.bfloat16)[None],
        grad_v_local[None],
        gain_q_all,
        gain_k_all,
    )


def solution(mesh):
    return jax.shard_map(
        local,
        mesh=mesh,
        in_specs=(
            P("dp", "seq", None),
            P("dp", "seq", None),
            P("dp", "seq", None),
            P("dp", "seq", None),
            P(),
            P(),
        ),
        out_specs=(P("dp", "seq", None), P("dp", "seq", None), P("dp", "seq", None), P(), P()),
        check_vma=False,
    )
```

profile of v0, /device:TPU:25, one launch (start us, length us, event | category | flops | bytes accessed | tf_op | source)
XLA Modules:
  0.0 255.1 jit_solution(8285778720912913618)
XLA Ops:
  3.4 4.2 %collective-permute-start = (bf16[256,512]{0,1:T(8,128)(2,1)S(1)}, bf16[256,512]{0,1:T(8,128)(2,1)}, u32[]{:S(2)}, u32[]{:S(2)}) collective-permute-start(bf16[256,512]{0,1:T(8,128)(2,1)S(1)} %bitcast.80), channel_id=1, source_target_pairs={{0,32},{8,40},{16,48},{24,56},{32,64},{40,72},{48,80},{56,88},{64,... | collective-permute-start | bytes 786440 | tf_op jit(solution)/shard_map/ppermute | solution.py:17
  7.6 4.8 %collective-permute-start.1 = (bf16[256,512]{0,1:T(8,128)(2,1)S(1)}, bf16[256,512]{0,1:T(8,128)(2,1)}, u32[]{:S(2)}, u32[]{:S(2)}) collective-permute-start(bf16[256,512]{0,1:T(8,128)(2,1)S(1)} %bitcast.81), channel_id=1, source_target_pairs={{0,24},{8,32},{16,40},{24,48},{32,56},{40,64},{48,72},{56,80},{64,... | collective-permute-start | bytes 786440 | tf_op jit(solution)/shard_map/ppermute | solution.py:17
  12.4 3.2 %collective-permute-start.2 = (bf16[256,512]{0,1:T(8,128)(2,1)S(1)}, bf16[256,512]{0,1:T(8,128)(2,1)}, u32[]{:S(2)}, u32[]{:S(2)}) collective-permute-start(bf16[256,512]{0,1:T(8,128)(2,1)S(1)} %bitcast.82), channel_id=1, source_target_pairs={{0,16},{8,24},{16,32},{24,40},{32,48},{40,56},{48,64},{56,72},{64,... | collective-permute-start | bytes 786440 | tf_op jit(solution)/shard_map/ppermute | solution.py:17
  15.6 1.9 collective-permute-start.3
  17.7 4.8 %collective-permute-start.4 = (bf16[256,512]{0,1:T(8,128)(2,1)S(1)}, bf16[256,512]{0,1:T(8,128)(2,1)}, u32[]{:S(2)}, u32[]{:S(2)}) collective-permute-start(bf16[256,512]{0,1:T(8,128)(2,1)S(1)} %bitcast.85), channel_id=1, source_target_pairs={{0,32},{8,40},{16,48},{24,56},{32,64},{40,72},{48,80},{56,88},{64,... | collective-permute-start | bytes 786440 | tf_op jit(solution)/shard_map/ppermute | solution.py:17
  28.8 4.0 %collective-permute-start.5 = (bf16[256,512]{0,1:T(8,128)(2,1)S(1)}, bf16[256,512]{0,1:T(8,128)(2,1)S(1)}, u32[]{:S(2)}, u32[]{:S(2)}) collective-permute-start(bf16[256,512]{0,1:T(8,128)(2,1)S(1)} %bitcast.87), channel_id=1, source_target_pairs={{0,24},{8,32},{16,40},{24,48},{32,56},{40,64},{48,72},{56,80},{64,... | collective-permute-start | bytes 786440 | tf_op jit(solution)/shard_map/ppermute | solution.py:17
  33.8 3.2 %collective-permute-start.6 = (bf16[256,512]{0,1:T(8,128)(2,1)S(1)}, bf16[256,512]{0,1:T(8,128)(2,1)}, u32[]{:S(2)}, u32[]{:S(2)}) collective-permute-start(bf16[256,512]{0,1:T(8,128)(2,1)S(1)} %bitcast.88), channel_id=1, source_target_pairs={{0,16},{8,24},{16,32},{24,40},{32,48},{40,56},{48,64},{56,72},{64,... | collective-permute-start | bytes 786440 | tf_op jit(solution)/shard_map/ppermute | solution.py:17
  38.0 2.1 collective-permute-start.7
  52.9 3.0 %fusion.39 = (f32[2,2,256]{2,1,0:T(2,128)S(1)}, f32[2,2,256,1280]{2,3,1,0:T(8,128)S(1)}) fusion(bf16[1280,2,256,1]{0,2,3,1:T(8,128)(2,1)} %bitcast.94, bf16[256,2,2,256]{3,0,2,1:T(8,128)(2,1)} %bitcast.91, pred[256,1280]{0,1:T(8,128)(4,1)} %fusion.20), kind=kOutput, calls=%fused_computation.89 | convolution fusion | flops 675019776 | bytes 7409664 | tf_op jit(solution)/shard_map/tkgd,skd->kgts/dot_general | solution.py:89
  58.7 3.2 %fusion.15 = f32[2,1280,256,2]{2,1,3,0:T(8,128)} fusion(bf16[256,2,2,256]{0,3,2,1:T(8,128)(2,1)S(1)} %bitcast.76, bf16[1280,2,256]{2,0,1:T(8,128)(2,1)S(1)} %constant_dynamic-update-slice_fusion.5), kind=kOutput, calls=%fused_computation.20 | convolution fusion | flops 671088640 | bytes 7077888 | tf_op jit(solution)/shard_map/tkgd,skd->kgts/dot_general | solution.py:97
  61.9 10.9 %fusion.6 = f32[2,256,2,256]{3,1,2,0:T(8,128)} fusion(bf16[1280,2,256,1]{0,2,3,1:T(8,128)(2,1)} %bitcast.95, f32[2,1280,256,2]{2,1,3,0:T(8,128)} %fusion.15, f32[2,2,256,1280]{2,3,1,0:T(8,128)} %copy-done, f32[2,2,256]{2,1,0:T(2,128)S(1)} %log_add_fusion), kind=kOutput, calls=%fused_computation.13 | convolution fusion | flops 680265984 | bytes 12849152 | tf_op jit(solution)/shard_map/kgts,skd->tkgd/dot_general | solution.py:100
  72.7 11.7 %fusion.40 = (bf16[1280,2,256]{0,2,1:T(8,128)(2,1)}, f32[1280,2,256]{0,2,1:T(8,128)}) fusion(bf16[256,2,2,256]{3,0,2,1:T(8,128)(2,1)S(1)} %bitcast.92, f32[2,1280,256,2]{2,1,3,0:T(8,128)} %fusion.15, f32[2,2,256,1280]{2,3,1,0:T(8,128)} %copy-done, f32[2,2,256]{2,1,0:T(2,128)S(1)} %log_add_fusion), kind=kOutput, calls=%fused_computation.90 | convolution fusion | flops 680921344 | bytes 14946304 | tf_op jit(solution)/shard_map/kgts,tkgd->skd/dot_general | solution.py:103
  84.5 5.4 %fusion.41 = (bf16[1280,2,256]{0,2,1:T(8,128)(2,1)}, f32[1280,2,256]{0,2,1:T(8,128)}) fusion(bf16[256,2,2,256]{0,3,2,1:T(8,128)(2,1)S(1)} %bitcast.77, f32[2,2,256,1280]{2,3,1,0:T(8,128)} %copy-done, f32[2,2,256]{2,1,0:T(2,128)S(1)} %log_add_fusion), kind=kOutput, calls=%fused_computation.91 | convolution fusion | flops 674365440 | bytes 9703424 | tf_op jit(solution)/shard_map/kgts,tkgd->skd/dot_general | solution.py:104
  94.8 2.2 fusion.37
  98.9 1.9 collective-permute-start.10
  102.7 2.4 collective-permute-start.8
  107.8 2.1 fusion.36
  113.8 4.4 %collective-permute-start.13 = (bf16[256,2,256]{0,2,1:T(8,128)(2,1)S(1)}, bf16[256,2,256]{0,2,1:T(8,128)(2,1)S(1)}, u32[]{:S(2)}, u32[]{:S(2)}) collective-permute-start(bf16[256,2,256]{0,2,1:T(8,128)(2,1)S(1)} %get-tuple-element.39), channel_id=1, source_target_pairs={{16,0},{24,8},{32,16},{40,24},{48,32},{56,40},{64,48},{72,56},{80,... | collective-permute-start | bytes 786440 | tf_op jit(solution)/shard_map/ppermute | solution.py:17
  118.3 4.9 %collective-permute-done.9 = bf16[256,2,256]{0,2,1:T(8,128)(2,1)} collective-permute-done((bf16[256,2,256]{0,2,1:T(8,128)(2,1)}, bf16[256,2,256]{0,2,1:T(8,128)(2,1)}, u32[]{:S(2)}, u32[]{:S(2)}) %collective-permute-start.9) | collective-permute-done | bytes 262176 | tf_op jit(solution)/shard_map/ppermute | solution.py:17
  123.1 3.3 %collective-permute-start.12 = (bf16[256,2,256]{0,2,1:T(8,128)(2,1)S(1)}, bf16[256,2,256]{0,2,1:T(8,128)(2,1)S(1)}, u32[]{:S(2)}, u32[]{:S(2)}) collective-permute-start(bf16[256,2,256]{0,2,1:T(8,128)(2,1)S(1)} %get-tuple-element.36), channel_id=1, source_target_pairs={{8,0},{16,8},{24,16},{32,24},{40,32},{48,40},{56,48},{64,56},{72,6... | collective-permute-start | bytes 786440 | tf_op jit(solution)/shard_map/ppermute | solution.py:17
  126.4 4.4 %collective-permute-done.8 = bf16[256,2,256]{0,2,1:T(8,128)(2,1)} collective-permute-done((bf16[256,2,256]{0,2,1:T(8,128)(2,1)}, bf16[256,2,256]{0,2,1:T(8,128)(2,1)}, u32[]{:S(2)}, u32[]{:S(2)}) %collective-permute-start.8) | collective-permute-done | bytes 262176 | tf_op jit(solution)/shard_map/ppermute | solution.py:17
  134.0 6.7 %collective-permute-done.13 = bf16[256,2,256]{0,2,1:T(8,128)(2,1)S(1)} collective-permute-done((bf16[256,2,256]{0,2,1:T(8,128)(2,1)S(1)}, bf16[256,2,256]{0,2,1:T(8,128)(2,1)S(1)}, u32[]{:S(2)}, u32[]{:S(2)}) %collective-permute-start.13) | collective-permute-done | bytes 262176 | tf_op jit(solution)/shard_map/ppermute | solution.py:17
  140.7 5.9 %collective-permute-done.12 = bf16[256,2,256]{0,2,1:T(8,128)(2,1)S(1)} collective-permute-done((bf16[256,2,256]{0,2,1:T(8,128)(2,1)S(1)}, bf16[256,2,256]{0,2,1:T(8,128)(2,1)S(1)}, u32[]{:S(2)}, u32[]{:S(2)}) %collective-permute-start.12) | collective-permute-done | bytes 262176 | tf_op jit(solution)/shard_map/ppermute | solution.py:17
  148.6 106.5 %all-reduce.4 = (f32[256]{0:T(256)}, f32[256]{0:T(256)}) all-reduce(f32[256]{0:T(256)S(1)} %copy-done.15, f32[256]{0:T(256)S(1)} %get-tuple-element.32), channel_id=1, replica_groups=mesh['seq'=64,'dp'=8] {'seq','dp'}, use_global_device_ids=true, to_apply=%region_8.9 | all-reduce | flops 512 | bytes 4096 | tf_op jit(solution)/shard_map/psum | solution.py:117
  (108 shorter events, 46.8 us)
Async XLA Ops:
  0.6 16.9 %copy-start.9 = (bf16[1,256,512]{2,1,0:T(8,128)(2,1)S(1)}, bf16[1,256,512]{2,1,0:T(8,128)(2,1)}, u32[]{:S(2)}) copy-start(bf16[1,256,512]{2,1,0:T(8,128)(2,1)} %param.8) | copy-start | bytes 786436
  0.7 22.1 %copy-start.7 = (bf16[1,256,1024]{2,1,0:T(8,128)(2,1)S(1)}, bf16[1,256,1024]{2,1,0:T(8,128)(2,1)}, u32[]{:S(2)}) copy-start(bf16[1,256,1024]{2,1,0:T(8,128)(2,1)} %param.6) | copy-start | bytes 1572868
  3.2 20.6 %copy-start.12 = (f32[256]{0:T(256)S(1)}, f32[256]{0:T(256)}, u32[]{:S(2)}) copy-start(f32[256]{0:T(256)} %param.10) | copy-start | bytes 3076
  3.4 25.5 %collective-permute-start = (bf16[256,512]{0,1:T(8,128)(2,1)S(1)}, bf16[256,512]{0,1:T(8,128)(2,1)}, u32[]{:S(2)}, u32[]{:S(2)}) collective-permute-start(bf16[256,512]{0,1:T(8,128)(2,1)S(1)} %bitcast.80), channel_id=1, source_target_pairs={{0,32},{8,40},{16,48},{24,56},{32,64},{40,72},{48,80},{56,88},{64,... | collective-permute-start | bytes 786440 | tf_op jit(solution)/shard_map/ppermute | solution.py:17
  7.6 26.2 %collective-permute-start.1 = (bf16[256,512]{0,1:T(8,128)(2,1)S(1)}, bf16[256,512]{0,1:T(8,128)(2,1)}, u32[]{:S(2)}, u32[]{:S(2)}) collective-permute-start(bf16[256,512]{0,1:T(8,128)(2,1)S(1)} %bitcast.81), channel_id=1, source_target_pairs={{0,24},{8,32},{16,40},{24,48},{32,56},{40,64},{48,72},{56,80},{64,... | collective-permute-start | bytes 786440 | tf_op jit(solution)/shard_map/ppermute | solution.py:17
  12.4 25.6 %collective-permute-start.2 = (bf16[256,512]{0,1:T(8,128)(2,1)S(1)}, bf16[256,512]{0,1:T(8,128)(2,1)}, u32[]{:S(2)}, u32[]{:S(2)}) collective-permute-start(bf16[256,512]{0,1:T(8,128)(2,1)S(1)} %bitcast.82), channel_id=1, source_target_pairs={{0,16},{8,24},{16,32},{24,40},{32,48},{40,56},{48,64},{56,72},{64,... | collective-permute-start | bytes 786440 | tf_op jit(solution)/shard_map/ppermute | solution.py:17
  15.6 25.5 %collective-permute-start.3 = (bf16[256,512]{0,1:T(8,128)(2,1)S(1)}, bf16[256,512]{0,1:T(8,128)(2,1)}, u32[]{:S(2)}, u32[]{:S(2)}) collective-permute-start(bf16[256,512]{0,1:T(8,128)(2,1)S(1)} %bitcast.83), channel_id=1, source_target_pairs={{0,8},{8,16},{16,24},{24,32},{32,40},{40,48},{48,56},{56,64},{64,7... | collective-permute-start | bytes 786440 | tf_op jit(solution)/shard_map/ppermute | solution.py:17
  17.7 24.4 %collective-permute-start.4 = (bf16[256,512]{0,1:T(8,128)(2,1)S(1)}, bf16[256,512]{0,1:T(8,128)(2,1)}, u32[]{:S(2)}, u32[]{:S(2)}) collective-permute-start(bf16[256,512]{0,1:T(8,128)(2,1)S(1)} %bitcast.85), channel_id=1, source_target_pairs={{0,32},{8,40},{16,48},{24,56},{32,64},{40,72},{48,80},{56,88},{64,... | collective-permute-start | bytes 786440 | tf_op jit(solution)/shard_map/ppermute | solution.py:17
  28.8 16.1 %collective-permute-start.5 = (bf16[256,512]{0,1:T(8,128)(2,1)S(1)}, bf16[256,512]{0,1:T(8,128)(2,1)S(1)}, u32[]{:S(2)}, u32[]{:S(2)}) collective-permute-start(bf16[256,512]{0,1:T(8,128)(2,1)S(1)} %bitcast.87), channel_id=1, source_target_pairs={{0,24},{8,32},{16,40},{24,48},{32,56},{40,64},{48,72},{56,80},{64,... | collective-permute-start | bytes 786440 | tf_op jit(solution)/shard_map/ppermute | solution.py:17
  33.8 14.7 %collective-permute-start.6 = (bf16[256,512]{0,1:T(8,128)(2,1)S(1)}, bf16[256,512]{0,1:T(8,128)(2,1)}, u32[]{:S(2)}, u32[]{:S(2)}) collective-permute-start(bf16[256,512]{0,1:T(8,128)(2,1)S(1)} %bitcast.88), channel_id=1, source_target_pairs={{0,16},{8,24},{16,32},{24,40},{32,48},{40,56},{48,64},{56,72},{64,... | collective-permute-start | bytes 786440 | tf_op jit(solution)/shard_map/ppermute | solution.py:17
  38.0 13.8 %collective-permute-start.7 = (bf16[256,512]{0,1:T(8,128)(2,1)S(1)}, bf16[256,512]{0,1:T(8,128)(2,1)}, u32[]{:S(2)}, u32[]{:S(2)}) collective-permute-start(bf16[256,512]{0,1:T(8,128)(2,1)S(1)} %bitcast.89), channel_id=1, source_target_pairs={{0,8},{8,16},{16,24},{24,32},{32,40},{40,48},{48,56},{56,64},{64,7... | collective-permute-start | bytes 786440 | tf_op jit(solution)/shard_map/ppermute | solution.py:17
  55.9 2.8 %copy-start.5 = (bf16[256,2,256]{2,0,1:T(8,128)(2,1)S(1)}, bf16[256,2,256]{2,0,1:T(8,128)(2,1)}, u32[]{:S(2)}) copy-start(bf16[256,2,256]{2,0,1:T(8,128)(2,1)} %copy.114) | copy-start | bytes 786436
  61.9 10.9 %copy-start.8 = (bf16[256,4,256]{2,0,1:T(8,128)(2,1)S(1)}, bf16[256,4,256]{2,0,1:T(8,128)(2,1)}, u32[]{:S(2)}) copy-start(bf16[256,4,256]{2,0,1:T(8,128)(2,1)} %copy.106) | copy-start | bytes 1572868
  84.4 5.4 %copy-start.4 = (f32[2,256,2,256]{3,1,2,0:T(8,128)S(1)}, f32[2,256,2,256]{3,1,2,0:T(8,128)}, u32[]{:S(2)}) copy-start(f32[2,256,2,256]{3,1,2,0:T(8,128)} %fusion.6) | copy-start | bytes 3145732
  96.9 14.9 %collective-permute-start.11 = (bf16[256,2,256]{0,2,1:T(8,128)(2,1)}, bf16[256,2,256]{0,2,1:T(8,128)(2,1)}, u32[]{:S(2)}, u32[]{:S(2)}) collective-permute-start(bf16[256,2,256]{0,2,1:T(8,128)(2,1)} %get-tuple-element.41), channel_id=1, source_target_pairs={{32,0},{40,8},{48,16},{56,24},{64,32},{72,40},{80,48},{88,56},{96,... | collective-permute-start | bytes 786440 | tf_op jit(solution)/shard_map/ppermute | solution.py:17
  98.9 14.9 %collective-permute-start.10 = (bf16[256,2,256]{0,2,1:T(8,128)(2,1)}, bf16[256,2,256]{0,2,1:T(8,128)(2,1)}, u32[]{:S(2)}, u32[]{:S(2)}) collective-permute-start(bf16[256,2,256]{0,2,1:T(8,128)(2,1)} %get-tuple-element.42), channel_id=1, source_target_pairs={{24,0},{32,8},{40,16},{48,24},{56,32},{64,40},{72,48},{80,56},{88,... | collective-permute-start | bytes 786440 | tf_op jit(solution)/shard_map/ppermute | solution.py:17
  100.8 22.4 %collective-permute-start.9 = (bf16[256,2,256]{0,2,1:T(8,128)(2,1)}, bf16[256,2,256]{0,2,1:T(8,128)(2,1)}, u32[]{:S(2)}, u32[]{:S(2)}) collective-permute-start(bf16[256,2,256]{0,2,1:T(8,128)(2,1)} %get-tuple-element.43), channel_id=1, source_target_pairs={{16,0},{24,8},{32,16},{40,24},{48,32},{56,40},{64,48},{72,56},{80,... | collective-permute-start | bytes 786440 | tf_op jit(solution)/shard_map/ppermute | solution.py:17
  102.7 28.1 %collective-permute-start.8 = (bf16[256,2,256]{0,2,1:T(8,128)(2,1)}, bf16[256,2,256]{0,2,1:T(8,128)(2,1)}, u32[]{:S(2)}, u32[]{:S(2)}) collective-permute-start(bf16[256,2,256]{0,2,1:T(8,128)(2,1)} %get-tuple-element.40), channel_id=1, source_target_pairs={{8,0},{16,8},{24,16},{32,24},{40,32},{48,40},{56,48},{64,56},{72,6... | collective-permute-start | bytes 786440 | tf_op jit(solution)/shard_map/ppermute | solution.py:17
  107.8 24.5 %copy-start.14 = (f32[256]{0:T(256)S(1)}, f32[256]{0:T(256)}, u32[]{:S(2)}) copy-start(f32[256]{0:T(256)} %param.11) | copy-start | bytes 3076
  109.9 23.7 %collective-permute-start.15 = (bf16[256,2,256]{0,2,1:T(8,128)(2,1)}, bf16[256,2,256]{0,2,1:T(8,128)(2,1)S(1)}, u32[]{:S(2)}, u32[]{:S(2)}) collective-permute-start(bf16[256,2,256]{0,2,1:T(8,128)(2,1)} %get-tuple-element.37), channel_id=1, source_target_pairs={{32,0},{40,8},{48,16},{56,24},{64,32},{72,40},{80,48},{88,56},{96,... | collective-permute-start | bytes 786440 | tf_op jit(solution)/shard_map/ppermute | solution.py:17
  111.9 22.1 %collective-permute-start.14 = (bf16[256,2,256]{0,2,1:T(8,128)(2,1)}, bf16[256,2,256]{0,2,1:T(8,128)(2,1)S(1)}, u32[]{:S(2)}, u32[]{:S(2)}) collective-permute-start(bf16[256,2,256]{0,2,1:T(8,128)(2,1)} %get-tuple-element.38), channel_id=1, source_target_pairs={{24,0},{32,8},{40,16},{48,24},{56,32},{64,40},{72,48},{80,56},{88,... | collective-permute-start | bytes 786440 | tf_op jit(solution)/shard_map/ppermute | solution.py:17
  113.8 26.9 %collective-permute-start.13 = (bf16[256,2,256]{0,2,1:T(8,128)(2,1)S(1)}, bf16[256,2,256]{0,2,1:T(8,128)(2,1)S(1)}, u32[]{:S(2)}, u32[]{:S(2)}) collective-permute-start(bf16[256,2,256]{0,2,1:T(8,128)(2,1)S(1)} %get-tuple-element.39), channel_id=1, source_target_pairs={{16,0},{24,8},{32,16},{40,24},{48,32},{56,40},{64,48},{72,56},{80,... | collective-permute-start | bytes 786440 | tf_op jit(solution)/shard_map/ppermute | solution.py:17
  123.1 23.5 %collective-permute-start.12 = (bf16[256,2,256]{0,2,1:T(8,128)(2,1)S(1)}, bf16[256,2,256]{0,2,1:T(8,128)(2,1)S(1)}, u32[]{:S(2)}, u32[]{:S(2)}) collective-permute-start(bf16[256,2,256]{0,2,1:T(8,128)(2,1)S(1)} %get-tuple-element.36), channel_id=1, source_target_pairs={{8,0},{16,8},{24,16},{32,24},{40,32},{48,40},{56,48},{64,56},{72,6... | collective-permute-start | bytes 786440 | tf_op jit(solution)/shard_map/ppermute | solution.py:17
  132.4 16.2 %copy-start.15 = (f32[256]{0:T(256)S(1)}, f32[256]{0:T(256)}, u32[]{:S(2)}) copy-start(f32[256]{0:T(256)} %get-tuple-element.30) | copy-start | bytes 3076
  (8 other events, 17.0 us)
where the time goes:
time: 259 us; the launch traced here: 255 us
  blocking collectives  106 us (41%)
  starting transfers between devices  47.9 us (18%)
  matrix products  34.2 us (13%)
  local copies, waits for them, and re-layouts  28.6 us (11%)
  waiting for transfers between devices  24.8 us (10%)
  other arithmetic  11.9 us (5%)
    psum x1, blocking collectives, local(): lax.psum((gain_q_local, gain_k_local), ('seq', 'dp'))  106 us
    ppermute x16, starting transfers between devices, from_behind(): return lax.ppermute(array, axis, pairs)  47.9 us
    ppermute x16, waiting for transfers between devices, from_behind(): return lax.ppermute(array, axis, pairs)  24.8 us
    dot_general x1, matrix products, local(): jnp.einsum('kgts,tkgd->skd', dscores, q_heads, preferred_element_type=jnp...  11.7 us
    unnamed x45, local copies, waits for them, and re-layouts  11.5 us
    dot_general x1, matrix products, local(): jnp.einsum('kgts,skd->tkgd', dscores, k_heads, preferred_element_type=jnp...  10.9 us
    concatenate x6, local copies, waits for them, and re-layouts, local(): value_rows = jnp.concatenate(halo_v + [v_local], axis=0)  5.89 us
    dot_general x1, matrix products, local(): jnp.einsum('kgts,tkgd->skd', weights_b, do_heads, preferred_element_type=...  5.41 us
  transfers between devices with their start and end apart: 16, of which 7 were waited for; matrix products, arithmetic and copies ran while one was open for 9% of the time, Pallas kernels for 0%

commit v1 on v0

--- a/solution.py
+++ b/solution.py
@@ -1,6 +1,8 @@
 import jax
 import jax.numpy as jnp
 from jax import lax
+from jax.experimental import pallas as pl
+from jax.experimental.pallas import tpu as pltpu
 from jax.sharding import PartitionSpec as P
 
 WINDOW = 1024
@@ -11,10 +13,103 @@
 MASKED = -1e30
 
 
-def from_behind(array, axis, by):
-    count = lax.axis_size(axis)
+def from_behind(array, by):
+    count = lax.axis_size("seq")
     pairs = [(i, i + by) for i in range(count) if 0 <= i + by < count]
-    return lax.ppermute(array, axis, pairs)
+    return lax.ppermute(array, "seq", pairs)
+
+
+def core_swap(array):
+    count = lax.axis_size("seq")
+    return lax.ppermute(array, "seq", [(i, i ^ 1) for i in range(count)])
+
+
+LOW = 8
+X_SIZE = 4
+
+
+def gain_sum_kernel(seq_size, dp_size, x_ref, o_ref, slots_a, slots_b, slots_c, part_b, part_c, send_sem, recv_sem):
+    seq = lax.axis_index("seq")
+    dp = lax.axis_index("dp")
+    z_lo_size = seq_size // LOW
+    z_size = z_lo_size * (dp_size // X_SIZE)
+    low = lax.rem(seq, LOW)
+    z_lo = lax.div(seq, LOW)
+    x_pos = lax.rem(dp, X_SIZE)
+    z_pos = lax.div(dp, X_SIZE) * z_lo_size + z_lo
+
+    def peer_a(k):
+        return {"seq": z_lo * LOW + lax.rem(low + k, LOW), "dp": dp}
+
+    def peer_b(k):
+        return {"seq": seq, "dp": dp - x_pos + lax.rem(x_pos + k, X_SIZE)}
+
+    def peer_c(k):
+        z_other = lax.rem(z_pos + k, z_size)
+        return {
+            "seq": lax.rem(z_other, z_lo_size) * LOW + low,
+            "dp": lax.div(z_other, z_lo_size) * X_SIZE + x_pos,
+        }
+
+    stages = ((LOW, peer_a, low), (X_SIZE, peer_b, x_pos), (z_size, peer_c, z_pos))
+    barrier = pltpu.get_barrier_semaphore()
+    total = 0
+    for size, peer, _ in reversed(stages):
+        for k in range(1, size):
+            pl.semaphore_signal(barrier, inc=1, device_id=peer(k), device_id_type=pl.DeviceIdType.MESH)
+            total += 1
+    pl.semaphore_wait(barrier, total)
+
+    base = 0
+    sources = (x_ref, part_b, part_c)
+    results = (part_b, part_c, o_ref)
+    for (size, peer, mine), source, slots, result in zip(
+        stages, sources, (slots_a, slots_b, slots_c), results
+    ):
+        copies = []
+        for k in range(1, size):
+            copy = pltpu.make_async_remote_copy(
+                src_ref=source,
+                dst_ref=slots.at[k],
+                send_sem=send_sem.at[base + k - 1],
+                recv_sem=recv_sem.at[base + k - 1],
+                device_id=peer(k),
+                device_id_type=pl.DeviceIdType.MESH,
+            )
+            copy.start()
+            copies.append(copy)
+        slots[0] = source[...]
+        for copy in copies:
+            copy.wait()
+        acc = slots[lax.rem(mine + size, size)]
+        for j in range(1, size):
+            acc = acc + slots[lax.rem(mine - j + size, size)]
+        result[...] = acc
+        base += size - 1
+
+
+def gain_sum(gains):
+    seq_size = lax.axis_size("seq")
+    dp_size = lax.axis_size("dp")
+    z_size = seq_size // LOW * (dp_size // X_SIZE)
+    peers = LOW + X_SIZE + z_size - 3
+    return pl.pallas_call(
+        lambda *refs: gain_sum_kernel(seq_size, dp_size, *refs),
+        out_shape=jax.ShapeDtypeStruct(gains.shape, jnp.float32),
+        in_specs=[pl.BlockSpec(memory_space=pltpu.VMEM)],
+        out_specs=pl.BlockSpec(memory_space=pltpu.VMEM),
+        scratch_shapes=[
+            pltpu.VMEM((LOW,) + gains.shape, jnp.float32),
+            pltpu.VMEM((X_SIZE,) + gains.shape, jnp.float32),
+            pltpu.VMEM((z_size,) + gains.shape, jnp.float32),
+            pltpu.VMEM(gains.shape, jnp.float32),
+            pltpu.VMEM(gains.shape, jnp.float32),
+            pltpu.SemaphoreType.DMA((peers,)),
+            pltpu.SemaphoreType.DMA((peers,)),
+        ],
+        compiler_params=pltpu.CompilerParams(collective_id=0, has_side_effects=True),
+        name="gain_sum",
+    )(gains)
 
 
 def rope_tables(positions, head_size):
@@ -69,14 +164,17 @@
     )
     q_rot = q_rot32.astype(jnp.bfloat16)
     k_rot = k_rot32.astype(jnp.bfloat16)
-    halo_k = []
-    halo_v = []
-    for offset in range(reach_dev, 0, -1):
-        received = from_behind((k_rot, v_local), "seq", offset)
-        halo_k.append(received[0])
-        halo_v.append(received[1])
-    key_rows = jnp.concatenate(halo_k + [k_rot], axis=0)
-    value_rows = jnp.concatenate(halo_v + [v_local], axis=0)
+    first_core = lax.rem(lax.axis_index("seq"), 2) == 0
+
+    def halo(own):
+        two = from_behind(own, 2)
+        four = from_behind(two, 2)
+        one = core_swap(jnp.where(first_core, own, two))
+        three = core_swap(jnp.where(first_core, two, four))
+        return jnp.concatenate([four, three, two, one, own], axis=0)
+
+    key_rows = halo(k_rot)
+    value_rows = halo(v_local)
     q_heads = q_rot.reshape(rows_here, pair_heads, group_size, head_size)
     k_heads = key_rows.reshape(key_span, pair_heads, head_size)
     v_heads = value_rows.reshape(key_span, pair_heads, head_size)
@@ -102,19 +200,29 @@
     ).reshape(rows_here, query_heads * head_size)
     dk_all = jnp.einsum("kgts,tkgd->skd", dscores, q_heads, preferred_element_type=jnp.float32)
     dv_all = jnp.einsum("kgts,tkgd->skd", weights_b, do_heads, preferred_element_type=jnp.float32)
-    dk_own = dk_all[WINDOW:]
-    dv_own = dv_all[WINDOW:]
-    for offset in range(1, reach_dev + 1):
-        low_row = (reach_dev - offset) * rows_here
-        sent_k = dk_all[low_row : low_row + rows_here].astype(jnp.bfloat16)
-        sent_v = dv_all[low_row : low_row + rows_here].astype(jnp.bfloat16)
-        received = from_behind((sent_k, sent_v), "seq", -offset)
-        dk_own = dk_own + received[0].astype(jnp.float32)
-        dv_own = dv_own + received[1].astype(jnp.float32)
+
+    def collect(terms):
+        def block(offset):
+            low_row = (reach_dev - offset) * rows_here
+            return terms[low_row : low_row + rows_here]
+
+        one = core_swap(block(1).astype(jnp.bfloat16)).astype(jnp.float32)
+        three = core_swap(block(3).astype(jnp.bfloat16)).astype(jnp.float32)
+        own = block(0) + jnp.where(first_core, one, 0.0)
+        two = block(2) + jnp.where(first_core, three, one)
+        four = block(4) + jnp.where(first_core, 0.0, three)
+        from_four = from_behind(four.astype(jnp.bfloat16), -2).astype(jnp.float32)
+        from_two = from_behind((two + from_four).astype(jnp.bfloat16), -2)
+        return own + from_two.astype(jnp.float32)
+
+    dk_own = collect(dk_all)
+    dv_own = collect(dv_all)
     dk_rot = dk_own.reshape(rows_here, pair_heads * head_size)
     grad_q_local, gain_q_local = q_back(dq_rot)
     grad_k_local, gain_k_local = k_back(dk_rot)
-    gain_q_all, gain_k_all = lax.psum((gain_q_local, gain_k_local), ("seq", "dp"))
+    gains = jnp.concatenate([gain_q_local, gain_k_local]).reshape(4, 128)
+    gains = gain_sum(jnp.pad(gains, ((0, 4), (0, 0))))[:4].reshape(2, head_size)
+    gain_q_all, gain_k_all = gains[0], gains[1]
     grad_v_local = dv_own.reshape(rows_here, pair_heads * head_size).astype(jnp.bfloat16)
     return (
         grad_q_local.astype(jnp.bfloat16)[None],

time: 259 us -> 184 us (0.71)
  the two profiles are of different devices: /device:TPU:25 before, /device:TPU:1 now
where the time goes in v1:
time: 184 us; the launch traced here: 182 us
  starting transfers between devices  40.1 us (22%)
  Pallas kernels  37 us (20%)
  matrix products  34.1 us (19%)
  local copies, waits for them, and re-layouts  33.5 us (18%)
  other arithmetic  24.9 us (14%)
  waiting for transfers between devices  11.8 us (6%)
    pallas_call x1, Pallas kernels, gain_sum(): pl.pallas_call(lambda *refs: gain_sum_kernel(seq_size, dp_size, *refs), o...  37 us
    ppermute x8, starting transfers between devices, core_swap(): return lax.ppermute(array, 'seq', [(i, i ^ 1) for i in range(count)])  20.6 us
    ppermute x8, starting transfers between devices, from_behind(): return lax.ppermute(array, 'seq', pairs)  19.5 us
    unnamed x39, local copies, waits for them, and re-layouts  13 us
    ppermute x8, waiting for transfers between devices, from_behind(): return lax.ppermute(array, 'seq', pairs)  11.8 us
    dot_general x1, matrix products, local(): jnp.einsum('kgts,tkgd->skd', dscores, q_heads, preferred_element_type=jnp...  11.8 us
    dot_general x1, matrix products, local(): jnp.einsum('kgts,skd->tkgd', dscores, k_heads, preferred_element_type=jnp...  10.9 us
    concatenate x7, local copies, waits for them, and re-layouts, halo(): return jnp.concatenate([four, three, two, one, own], axis=0)  7.33 us
  transfers between devices with their start and end apart: 16, of which 4 were waited for; matrix products, arithmetic and copies ran while one was open for 25% of the time, Pallas kernels for 0%

profile of v1, /device:TPU:1, one launch (start us, length us, event | category | flops | bytes accessed | tf_op | source)
XLA Modules:
  0.0 182.5 jit_solution(1063521022651913958)
XLA Ops:
  3.4 4.7 %collective-permute-start = (bf16[256,512]{0,1:T(8,128)(2,1)S(1)}, bf16[256,512]{0,1:T(8,128)(2,1)}, u32[]{:S(2)}, u32[]{:S(2)}) collective-permute-start(bf16[256,512]{0,1:T(8,128)(2,1)S(1)} %bitcast.88), channel_id=1, source_target_pairs={{0,16},{8,24},{16,32},{24,40},{32,48},{40,56},{48,64},{56,72},{64,... | collective-permute-start | bytes 786440 | tf_op jit(solution)/shard_map/ppermute | solution.py:19
  8.2 3.3 %collective-permute-start.4 = (bf16[256,512]{0,1:T(8,128)(2,1)S(1)}, bf16[256,512]{0,1:T(8,128)(2,1)}, u32[]{:S(2)}, u32[]{:S(2)}) collective-permute-start(bf16[256,512]{0,1:T(8,128)(2,1)S(1)} %bitcast.86), channel_id=1, source_target_pairs={{0,16},{8,24},{16,32},{24,40},{32,48},{40,56},{48,64},{56,72},{64,... | collective-permute-start | bytes 786440 | tf_op jit(solution)/shard_map/ppermute | solution.py:19
  15.6 2.9 %collective-permute-start.1 = (bf16[256,512]{0,1:T(8,128)(2,1)}, bf16[256,512]{0,1:T(8,128)(2,1)}, u32[]{:S(2)}, u32[]{:S(2)}) collective-permute-start(bf16[256,512]{0,1:T(8,128)(2,1)} %collective-permute-done), channel_id=1, source_target_pairs={{0,16},{8,24},{16,32},{24,40},{32,48},{40,56},{48,64},{56,72},{64,... | collective-permute-start | bytes 786440 | tf_op jit(solution)/shard_map/ppermute | solution.py:19
  19.7 3.2 %collective-permute-start.5 = (bf16[256,512]{0,1:T(8,128)(2,1)}, bf16[256,512]{0,1:T(8,128)(2,1)}, u32[]{:S(2)}, u32[]{:S(2)}) collective-permute-start(bf16[256,512]{0,1:T(8,128)(2,1)} %collective-permute-done.4), channel_id=1, source_target_pairs={{0,16},{8,24},{16,32},{24,40},{32,48},{40,56},{48,64},{56,72},{64,... | collective-permute-start | bytes 786440 | tf_op jit(solution)/shard_map/ppermute | solution.py:19
  27.3 1.8 broadcast_select_fusion.3
  29.1 5.4 %collective-permute-start.2 = (bf16[256,512]{0,1:T(8,128)(2,1)}, bf16[256,512]{0,1:T(8,128)(2,1)}, u32[]{:S(2)}, u32[]{:S(2)}) collective-permute-start(bf16[256,512]{0,1:T(8,128)(2,1)} %get-tuple-element.52), channel_id=1, source_target_pairs={{0,8},{8,0},{16,24},{24,16},{32,40},{40,32},{48,56},{56,48},{64,72... | collective-permute-start | bytes 786440 | tf_op jit(solution)/shard_map/ppermute | solution.py:24
  38.1 2.0 %collective-permute-start.6 = (bf16[256,512]{0,1:T(8,128)(2,1)S(1)}, bf16[256,512]{0,1:T(8,128)(2,1)S(1)}, u32[]{:S(2)}, u32[]{:S(2)}) collective-permute-start(bf16[256,512]{0,1:T(8,128)(2,1)S(1)} %get-tuple-element.49), channel_id=1, source_target_pairs={{0,8},{8,0},{16,24},{24,16},{32,40},{40,32},{48,56},{56,48},{64,72... | collective-permute-start | bytes 786440 | tf_op jit(solution)/shard_map/ppermute | solution.py:24
  40.2 2.4 %collective-permute-start.7 = (bf16[256,512]{0,1:T(8,128)(2,1)}, bf16[256,512]{0,1:T(8,128)(2,1)}, u32[]{:S(2)}, u32[]{:S(2)}) collective-permute-start(bf16[256,512]{0,1:T(8,128)(2,1)} %get-tuple-element.48), channel_id=1, source_target_pairs={{0,8},{8,0},{16,24},{24,16},{32,40},{40,32},{48,56},{56,48},{64,72... | collective-permute-start | bytes 786440 | tf_op jit(solution)/shard_map/ppermute | solution.py:24
  46.0 1.8 broadcast_select_fusion.2
  47.8 2.1 %collective-permute-start.3 = (bf16[256,512]{0,1:T(8,128)(2,1)}, bf16[256,512]{0,1:T(8,128)(2,1)}, u32[]{:S(2)}, u32[]{:S(2)}) collective-permute-start(bf16[256,512]{0,1:T(8,128)(2,1)} %get-tuple-element.50), channel_id=1, source_target_pairs={{0,8},{8,0},{16,24},{24,16},{32,40},{40,32},{48,56},{56,48},{64,72... | collective-permute-start | bytes 786440 | tf_op jit(solution)/shard_map/ppermute | solution.py:24
  57.4 4.6 %fusion.15 = f32[2,1280,256,2]{2,1,3,0:T(8,128)} fusion(bf16[256,2,2,256]{0,3,2,1:T(8,128)(2,1)S(1)} %bitcast.84, bf16[1280,2,256]{2,0,1:T(8,128)(2,1)} %constant_dynamic-update-slice_fusion.5), kind=kOutput, calls=%fused_computation.20 | convolution fusion | flops 671088640 | bytes 7077888 | tf_op jit(solution)/shard_map/tkgd,skd->kgts/dot_general | solution.py:195
  66.9 10.9 %fusion.6 = f32[2,256,2,256]{3,1,2,0:T(8,128)} fusion(bf16[1280,2,256,1]{0,2,3,1:T(8,128)(2,1)} %bitcast.97, f32[2,1280,256,2]{2,1,3,0:T(8,128)} %fusion.15, f32[2,2,256,1280]{2,3,1,0:T(8,128)} %copy-done, f32[2,2,256]{2,1,0:T(2,128)S(1)} %log_add_fusion), kind=kOutput, calls=%fused_computation.13 | convolution fusion | flops 680265984 | bytes 12849152 | tf_op jit(solution)/shard_map/kgts,skd->tkgd/dot_general | solution.py:198
  77.8 11.8 %fusion.48 = (bf16[1280,2,256]{0,2,1:T(8,128)(2,1)}, f32[1280,2,256]{0,2,1:T(8,128)}) fusion(bf16[256,2,2,256]{3,0,2,1:T(8,128)(2,1)S(1)} %bitcast.94, f32[2,1280,256,2]{2,1,3,0:T(8,128)} %fusion.15, f32[2,2,256,1280]{2,3,1,0:T(8,128)} %copy-done, f32[2,2,256]{2,1,0:T(2,128)S(1)} %log_add_fusion), kind=kOutput, calls=%fused_computation.110 | convolution fusion | flops 680921344 | bytes 14946304 | tf_op jit(solution)/shard_map/kgts,tkgd->skd/dot_general | solution.py:201
  89.6 5.3 %fusion.49 = (bf16[1280,2,256]{0,2,1:T(8,128)(2,1)}, f32[1280,2,256]{0,2,1:T(8,128)}) fusion(bf16[256,2,2,256]{0,3,2,1:T(8,128)(2,1)S(1)} %bitcast.85, f32[2,2,256,1280]{2,3,1,0:T(8,128)} %copy-done, f32[2,2,256]{2,1,0:T(2,128)S(1)} %log_add_fusion), kind=kOutput, calls=%fused_computation.111 | convolution fusion | flops 674365440 | bytes 9703424 | tf_op jit(solution)/shard_map/kgts,tkgd->skd/dot_general | solution.py:202
  100.7 2.4 %collective-permute-start.9 = (bf16[256,2,256]{0,2,1:T(8,128)(2,1)S(1)}, bf16[256,2,256]{0,2,1:T(8,128)(2,1)S(1)}, u32[]{:S(2)}, u32[]{:S(2)}) collective-permute-start(bf16[256,2,256]{0,2,1:T(8,128)(2,1)S(1)} %get-tuple-element.36), channel_id=1, source_target_pairs={{0,8},{8,0},{16,24},{24,16},{32,40},{40,32},{48,56},{56,48},{64,72... | collective-permute-start | bytes 786440 | tf_op jit(solution)/shard_map/ppermute | solution.py:24
  105.2 1.9 %collective-permute-start.8 = (bf16[256,2,256]{0,2,1:T(8,128)(2,1)}, bf16[256,2,256]{0,2,1:T(8,128)(2,1)}, u32[]{:S(2)}, u32[]{:S(2)}) collective-permute-start(bf16[256,2,256]{0,2,1:T(8,128)(2,1)} %get-tuple-element.37), channel_id=1, source_target_pairs={{0,8},{8,0},{16,24},{24,16},{32,40},{40,32},{48,56},{56,48},{64,72... | collective-permute-start | bytes 786440 | tf_op jit(solution)/shard_map/ppermute | solution.py:24
  107.1 1.9 %fusion.44 = (bf16[256,2,256]{0,2,1:T(8,128)(2,1)}, bf16[256,2,256]{0,2,1:T(8,128)(2,1)}) fusion(bf16[1280,2,256]{0,2,1:T(8,128)(2,1)} %get-tuple-element.62), kind=kLoop, calls=%fused_computation.106 | loop fusion | bytes 1048576 | tf_op jit(solution)/shard_map/slice | solution.py:207
  109.0 2.4 %collective-permute-start.13 = (bf16[256,2,256]{0,2,1:T(8,128)(2,1)}, bf16[256,2,256]{0,2,1:T(8,128)(2,1)}, u32[]{:S(2)}, u32[]{:S(2)}) collective-permute-start(bf16[256,2,256]{0,2,1:T(8,128)(2,1)} %get-tuple-element.34), channel_id=1, source_target_pairs={{0,8},{8,0},{16,24},{24,16},{32,40},{40,32},{48,56},{56,48},{64,72... | collective-permute-start | bytes 786440 | tf_op jit(solution)/shard_map/ppermute | solution.py:24
  111.4 1.9 %fusion.28 = bf16[256,2,256]{0,2,1:T(8,128)(2,1)} fusion(bf16[256,2,256]{0,2,1:T(8,128)(2,1)S(1)} %collective-permute-done.9, f32[1280,2,256]{0,2,1:T(8,128)} %get-tuple-element.61, pred[]{:T(512)S(6)} %eq.3), kind=kLoop, calls=%fused_computation.46 | loop fusion | flops 524288 | bytes 1048577 | tf_op jit(solution)/shard_map/convert_element_type | solution.py:214
  117.6 1.9 %collective-permute-start.12 = (bf16[256,2,256]{0,2,1:T(8,128)(2,1)}, bf16[256,2,256]{0,2,1:T(8,128)(2,1)S(1)}, u32[]{:S(2)}, u32[]{:S(2)}) collective-permute-start(bf16[256,2,256]{0,2,1:T(8,128)(2,1)} %get-tuple-element.35), channel_id=1, source_target_pairs={{0,8},{8,0},{16,24},{24,16},{32,40},{40,32},{48,56},{56,48},{64,72... | collective-permute-start | bytes 786440 | tf_op jit(solution)/shard_map/ppermute | solution.py:24
  126.2 5.4 %collective-permute-done.14 = bf16[256,2,256]{0,2,1:T(8,128)(2,1)S(1)} collective-permute-done((bf16[256,2,256]{0,2,1:T(8,128)(2,1)S(1)}, bf16[256,2,256]{0,2,1:T(8,128)(2,1)S(1)}, u32[]{:S(2)}, u32[]{:S(2)}) %collective-permute-start.14) | collective-permute-done | bytes 262176 | tf_op jit(solution)/shard_map/ppermute | solution.py:19
  134.1 3.1 %collective-permute-done.11 = bf16[256,2,256]{0,2,1:T(8,128)(2,1)S(1)} collective-permute-done((bf16[256,2,256]{0,2,1:T(8,128)(2,1)S(1)}, bf16[256,2,256]{0,2,1:T(8,128)(2,1)S(1)}, u32[]{:S(2)}, u32[]{:S(2)}) %collective-permute-start.11) | collective-permute-done | bytes 262176 | tf_op jit(solution)/shard_map/ppermute | solution.py:19
  139.7 1.9 %collective-permute-done.15 = bf16[256,2,256]{0,2,1:T(8,128)(2,1)S(1)} collective-permute-done((bf16[256,2,256]{0,2,1:T(8,128)(2,1)S(1)}, bf16[256,2,256]{0,2,1:T(8,128)(2,1)S(1)}, u32[]{:S(2)}, u32[]{:S(2)}) %collective-permute-start.15) | collective-permute-done | bytes 262176 | tf_op jit(solution)/shard_map/ppermute | solution.py:19
  144.2 37.0 %gain_sum.1 = f32[8,128]{1,0:T(8,128)} custom-call(f32[8,128]{1,0:T(8,128)} %select_maximum_fusion.refs_0_), custom_call_target="tpu_custom_call" | custom-call | tf_op jit(solution)/shard_map/gain_sum/pallas_call | solution.py:96
  (111 shorter events, 59.3 us)
Async XLA Ops:
  0.6 7.5 %copy-start.7 = (bf16[1,256,512]{2,1,0:T(8,128)(2,1)S(1)}, bf16[1,256,512]{2,1,0:T(8,128)(2,1)}, u32[]{:S(2)}) copy-start(bf16[1,256,512]{2,1,0:T(8,128)(2,1)} %param.8) | copy-start | bytes 786436
  0.6 10.9 %copy-start.4 = (bf16[1,256,1024]{2,1,0:T(8,128)(2,1)S(1)}, bf16[1,256,1024]{2,1,0:T(8,128)(2,1)}, u32[]{:S(2)}) copy-start(bf16[1,256,1024]{2,1,0:T(8,128)(2,1)} %param.6) | copy-start | bytes 1572868
  3.2 10.5 %copy-start.11 = (f32[256]{0:T(256)S(1)}, f32[256]{0:T(256)}, u32[]{:S(2)}) copy-start(f32[256]{0:T(256)} %param.10) | copy-start | bytes 3076
  3.4 12.2 %collective-permute-start = (bf16[256,512]{0,1:T(8,128)(2,1)S(1)}, bf16[256,512]{0,1:T(8,128)(2,1)}, u32[]{:S(2)}, u32[]{:S(2)}) collective-permute-start(bf16[256,512]{0,1:T(8,128)(2,1)S(1)} %bitcast.88), channel_id=1, source_target_pairs={{0,16},{8,24},{16,32},{24,40},{32,48},{40,56},{48,64},{56,72},{64,... | collective-permute-start | bytes 786440 | tf_op jit(solution)/shard_map/ppermute | solution.py:19
  8.2 11.5 %collective-permute-start.4 = (bf16[256,512]{0,1:T(8,128)(2,1)S(1)}, bf16[256,512]{0,1:T(8,128)(2,1)}, u32[]{:S(2)}, u32[]{:S(2)}) collective-permute-start(bf16[256,512]{0,1:T(8,128)(2,1)S(1)} %bitcast.86), channel_id=1, source_target_pairs={{0,16},{8,24},{16,32},{24,40},{32,48},{40,56},{48,64},{56,72},{64,... | collective-permute-start | bytes 786440 | tf_op jit(solution)/shard_map/ppermute | solution.py:19
  15.6 11.7 %collective-permute-start.1 = (bf16[256,512]{0,1:T(8,128)(2,1)}, bf16[256,512]{0,1:T(8,128)(2,1)}, u32[]{:S(2)}, u32[]{:S(2)}) collective-permute-start(bf16[256,512]{0,1:T(8,128)(2,1)} %collective-permute-done), channel_id=1, source_target_pairs={{0,16},{8,24},{16,32},{24,40},{32,48},{40,56},{48,64},{56,72},{64,... | collective-permute-start | bytes 786440 | tf_op jit(solution)/shard_map/ppermute | solution.py:19
  19.7 14.8 %collective-permute-start.5 = (bf16[256,512]{0,1:T(8,128)(2,1)}, bf16[256,512]{0,1:T(8,128)(2,1)}, u32[]{:S(2)}, u32[]{:S(2)}) collective-permute-start(bf16[256,512]{0,1:T(8,128)(2,1)} %collective-permute-done.4), channel_id=1, source_target_pairs={{0,16},{8,24},{16,32},{24,40},{32,48},{40,56},{48,64},{56,72},{64,... | collective-permute-start | bytes 786440 | tf_op jit(solution)/shard_map/ppermute | solution.py:19
  29.1 15.2 %collective-permute-start.2 = (bf16[256,512]{0,1:T(8,128)(2,1)}, bf16[256,512]{0,1:T(8,128)(2,1)}, u32[]{:S(2)}, u32[]{:S(2)}) collective-permute-start(bf16[256,512]{0,1:T(8,128)(2,1)} %get-tuple-element.52), channel_id=1, source_target_pairs={{0,8},{8,0},{16,24},{24,16},{32,40},{40,32},{48,56},{56,48},{64,72... | collective-permute-start | bytes 786440 | tf_op jit(solution)/shard_map/ppermute | solution.py:24
  38.1 18.5 %copy-start.2 = (bf16[256,2,256]{2,0,1:T(8,128)(2,1)S(1)}, bf16[256,2,256]{2,0,1:T(8,128)(2,1)}, u32[]{:S(2)}) copy-start(bf16[256,2,256]{2,0,1:T(8,128)(2,1)} %copy.117) | copy-start | bytes 786436
  38.1 11.8 %collective-permute-start.6 = (bf16[256,512]{0,1:T(8,128)(2,1)S(1)}, bf16[256,512]{0,1:T(8,128)(2,1)S(1)}, u32[]{:S(2)}, u32[]{:S(2)}) collective-permute-start(bf16[256,512]{0,1:T(8,128)(2,1)S(1)} %get-tuple-element.49), channel_id=1, source_target_pairs={{0,8},{8,0},{16,24},{24,16},{32,40},{40,32},{48,56},{56,48},{64,72... | collective-permute-start | bytes 786440 | tf_op jit(solution)/shard_map/ppermute | solution.py:24
  40.2 11.6 %collective-permute-start.7 = (bf16[256,512]{0,1:T(8,128)(2,1)}, bf16[256,512]{0,1:T(8,128)(2,1)}, u32[]{:S(2)}, u32[]{:S(2)}) collective-permute-start(bf16[256,512]{0,1:T(8,128)(2,1)} %get-tuple-element.48), channel_id=1, source_target_pairs={{0,8},{8,0},{16,24},{24,16},{32,40},{40,32},{48,56},{56,48},{64,72... | collective-permute-start | bytes 786440 | tf_op jit(solution)/shard_map/ppermute | solution.py:24
  47.8 14.2 %collective-permute-start.3 = (bf16[256,512]{0,1:T(8,128)(2,1)}, bf16[256,512]{0,1:T(8,128)(2,1)}, u32[]{:S(2)}, u32[]{:S(2)}) collective-permute-start(bf16[256,512]{0,1:T(8,128)(2,1)} %get-tuple-element.50), channel_id=1, source_target_pairs={{0,8},{8,0},{16,24},{24,16},{32,40},{40,32},{48,56},{56,48},{64,72... | collective-permute-start | bytes 786440 | tf_op jit(solution)/shard_map/ppermute | solution.py:24
  57.4 5.6 %copy-start.5 = (bf16[256,4,256]{2,0,1:T(8,128)(2,1)S(1)}, bf16[256,4,256]{2,0,1:T(8,128)(2,1)}, u32[]{:S(2)}) copy-start(bf16[256,4,256]{2,0,1:T(8,128)(2,1)} %copy.109) | copy-start | bytes 1572868
  57.4 5.6 %copy-start.6 = (pred[256,1280]{0,1:T(8,128)(4,1)S(1)}, pred[256,1280]{0,1:T(8,128)(4,1)}, u32[]{:S(2)}) copy-start(pred[256,1280]{0,1:T(8,128)(4,1)} %fusion.20) | copy-start | bytes 983044
  89.6 5.3 %copy-start.1 = (f32[2,256,2,256]{3,1,2,0:T(8,128)S(1)}, f32[2,256,2,256]{3,1,2,0:T(8,128)}, u32[]{:S(2)}) copy-start(f32[2,256,2,256]{3,1,2,0:T(8,128)} %fusion.6) | copy-start | bytes 3145732
  100.7 10.7 %collective-permute-start.9 = (bf16[256,2,256]{0,2,1:T(8,128)(2,1)S(1)}, bf16[256,2,256]{0,2,1:T(8,128)(2,1)S(1)}, u32[]{:S(2)}, u32[]{:S(2)}) collective-permute-start(bf16[256,2,256]{0,2,1:T(8,128)(2,1)S(1)} %get-tuple-element.36), channel_id=1, source_target_pairs={{0,8},{8,0},{16,24},{24,16},{32,40},{40,32},{48,56},{56,48},{64,72... | collective-permute-start | bytes 786440 | tf_op jit(solution)/shard_map/ppermute | solution.py:24
  105.2 16.8 %collective-permute-start.8 = (bf16[256,2,256]{0,2,1:T(8,128)(2,1)}, bf16[256,2,256]{0,2,1:T(8,128)(2,1)}, u32[]{:S(2)}, u32[]{:S(2)}) collective-permute-start(bf16[256,2,256]{0,2,1:T(8,128)(2,1)} %get-tuple-element.37), channel_id=1, source_target_pairs={{0,8},{8,0},{16,24},{24,16},{32,40},{40,32},{48,56},{56,48},{64,72... | collective-permute-start | bytes 786440 | tf_op jit(solution)/shard_map/ppermute | solution.py:24
  109.0 10.5 %collective-permute-start.13 = (bf16[256,2,256]{0,2,1:T(8,128)(2,1)}, bf16[256,2,256]{0,2,1:T(8,128)(2,1)}, u32[]{:S(2)}, u32[]{:S(2)}) collective-permute-start(bf16[256,2,256]{0,2,1:T(8,128)(2,1)} %get-tuple-element.34), channel_id=1, source_target_pairs={{0,8},{8,0},{16,24},{24,16},{32,40},{40,32},{48,56},{56,48},{64,72... | collective-permute-start | bytes 786440 | tf_op jit(solution)/shard_map/ppermute | solution.py:24
  113.3 10.1 %collective-permute-start.10 = (bf16[256,2,256]{0,2,1:T(8,128)(2,1)}, bf16[256,2,256]{0,2,1:T(8,128)(2,1)}, u32[]{:S(2)}, u32[]{:S(2)}) collective-permute-start(bf16[256,2,256]{0,2,1:T(8,128)(2,1)} %fusion.28), channel_id=1, source_target_pairs={{16,0},{24,8},{32,16},{40,24},{48,32},{56,40},{64,48},{72,56},{80,... | collective-permute-start | bytes 786440 | tf_op jit(solution)/shard_map/ppermute | solution.py:19
  117.6 8.6 %collective-permute-start.12 = (bf16[256,2,256]{0,2,1:T(8,128)(2,1)}, bf16[256,2,256]{0,2,1:T(8,128)(2,1)S(1)}, u32[]{:S(2)}, u32[]{:S(2)}) collective-permute-start(bf16[256,2,256]{0,2,1:T(8,128)(2,1)} %get-tuple-element.35), channel_id=1, source_target_pairs={{0,8},{8,0},{16,24},{24,16},{32,40},{40,32},{48,56},{56,48},{64,72... | collective-permute-start | bytes 786440 | tf_op jit(solution)/shard_map/ppermute | solution.py:24
  120.7 10.8 %collective-permute-start.14 = (bf16[256,2,256]{0,2,1:T(8,128)(2,1)S(1)}, bf16[256,2,256]{0,2,1:T(8,128)(2,1)S(1)}, u32[]{:S(2)}, u32[]{:S(2)}) collective-permute-start(bf16[256,2,256]{0,2,1:T(8,128)(2,1)S(1)} %fusion.36), channel_id=1, source_target_pairs={{16,0},{24,8},{32,16},{40,24},{48,32},{56,40},{64,48},{72,56},{80,... | collective-permute-start | bytes 786440 | tf_op jit(solution)/shard_map/ppermute | solution.py:19
  124.9 13.6 %copy-start.12 = (f32[256]{0:T(256)S(1)}, f32[256]{0:T(256)}, u32[]{:S(2)}) copy-start(f32[256]{0:T(256)} %param.11) | copy-start | bytes 3076
  124.9 12.3 %collective-permute-start.11 = (bf16[256,2,256]{0,2,1:T(8,128)(2,1)S(1)}, bf16[256,2,256]{0,2,1:T(8,128)(2,1)S(1)}, u32[]{:S(2)}, u32[]{:S(2)}) collective-permute-start(bf16[256,2,256]{0,2,1:T(8,128)(2,1)S(1)} %fusion.26), channel_id=1, source_target_pairs={{16,0},{24,8},{32,16},{40,24},{48,32},{56,40},{64,48},{72,56},{80,... | collective-permute-start | bytes 786440 | tf_op jit(solution)/shard_map/ppermute | solution.py:19
  132.8 8.8 %collective-permute-start.15 = (bf16[256,2,256]{0,2,1:T(8,128)(2,1)S(1)}, bf16[256,2,256]{0,2,1:T(8,128)(2,1)S(1)}, u32[]{:S(2)}, u32[]{:S(2)}) collective-permute-start(bf16[256,2,256]{0,2,1:T(8,128)(2,1)S(1)} %fusion.34), channel_id=1, source_target_pairs={{16,0},{24,8},{32,16},{40,24},{48,32},{56,40},{64,48},{72,56},{80,... | collective-permute-start | bytes 786440 | tf_op jit(solution)/shard_map/ppermute | solution.py:19
  (6 other events, 16.3 us)

commit v2 on v1

v2 whole, which is shorter than its diff:
```python
import jax
import jax.numpy as jnp
from jax import lax
from jax.experimental import pallas as pl
from jax.experimental.pallas import tpu as pltpu
from jax.sharding import PartitionSpec as P

WINDOW = 1024


EPS = 1e-06
ROPE_BASE = 10000.0
MASKED = -1e30
MESH = pl.DeviceIdType.MESH

LOW = 8
X_SIZE = 4


def rope_tables(positions, head_size):
    half_size = head_size // 2
    freqs = jnp.power(ROPE_BASE, -(2.0 * jnp.arange(half_size, dtype=jnp.float32)) / head_size)
    angles = positions.astype(jnp.float32)[:, None] * freqs[None, :]
    return (jnp.cos(angles), jnp.sin(angles))


def norm_rope(raw_ref, out_ref, gain_ref, cosine, sine):
    head_size = gain_ref.shape[1]
    half = head_size // 2
    for start in range(0, raw_ref.shape[1], head_size):
        x = raw_ref[:, start : start + head_size].astype(jnp.float32)
        scaled = x * lax.rsqrt(jnp.mean(x * x, axis=-1, keepdims=True) + EPS) * gain_ref[...]
        lower, upper = scaled[:, :half], scaled[:, half:]
        out_ref[:, start : start + half] = (lower * cosine - upper * sine).astype(out_ref.dtype)
        out_ref[:, start + half : start + head_size] = (upper * cosine + lower * sine).astype(
            out_ref.dtype
        )


def norm_rope_back(raw_ref, grad_ref, out_ref, gain_ref, cosine, sine):
    head_size = gain_ref.shape[1]
    half = head_size // 2
    gain_grad = jnp.zeros((1, head_size), jnp.float32)
    for start in range(0, raw_ref.shape[1], head_size):
        x = raw_ref[:, start : start + head_size].astype(jnp.float32)
        inverse = lax.rsqrt(jnp.mean(x * x, axis=-1, keepdims=True) + EPS)
        normed = x * inverse
        lower = grad_ref[:, start : start + half]
        upper = grad_ref[:, start + half : start + head_size]
        d_scaled = jnp.concatenate(
            [lower * cosine + upper * sine, upper * cosine - lower * sine], axis=-1
        )
        gain_grad = gain_grad + jnp.sum(d_scaled * normed, axis=0, keepdims=True)
        d_normed = d_scaled * gain_ref[...]
        along = jnp.mean(d_normed * normed, axis=-1, keepdims=True)
        out_ref[:, start : start + head_size] = (inverse * (d_normed - normed * along)).astype(
            out_ref.dtype
        )
    return gain_grad


def greet_neighbours(seq, count):
    barrier = pltpu.get_barrier_semaphore()
    pl.semaphore_signal(barrier, inc=1, device_id={"seq": other_core(seq)}, device_id_type=MESH)

    @pl.when(seq >= 2)
    def _():
        pl.semaphore_signal(barrier, inc=1, device_id={"seq": seq - 2}, device_id_type=MESH)

    @pl.when(seq + 2 < count)
    def _():
        pl.semaphore_signal(barrier, inc=1, device_id={"seq": seq + 2}, device_id_type=MESH)

    inside = (seq >= 2) & (seq + 2 < count)

    @pl.when(inside)
    def _():
        pl.semaphore_wait(barrier, 3)

    @pl.when(jnp.logical_not(inside))
    def _():
        pl.semaphore_wait(barrier, 2)


def other_core(seq):
    return seq + 1 - 2 * lax.rem(seq, 2)


def halo_kernel(
    count, q_ref, k_ref, v_ref, q_gain_ref, k_gain_ref, cos_ref, sin_ref,
    q_out, k_out, v_out, send_sem, recv_sem, copy_sem,
):
    seq = lax.axis_index("seq")
    core = lax.rem(seq, 2)
    cosine, sine = cos_ref[...], sin_ref[...]
    outs = (v_out, k_out)

    def send(which, source, target, hop, device):
        return pltpu.make_async_remote_copy(
            src_ref=outs[which].at[source],
            dst_ref=outs[which].at[target],
            send_sem=send_sem.at[which, hop],
            recv_sem=recv_sem.at[which, hop],
            device_id={"seq": device},
            device_id_type=MESH,
        )

    ahead = seq + 2
    beside = other_core(seq)
    local = pltpu.make_async_copy(v_ref, v_out.at[4], copy_sem)
    local.start()
    greet_neighbours(seq, count)
    local.wait()

    def send_own(which):
        @pl.when(ahead < count)
        def _():
            send(which, 4, 2, 0, ahead).start()

    send_own(0)
    norm_rope(k_ref, k_out.at[4], k_gain_ref, cosine, sine)
    send_own(1)
    for which in range(2):

        @pl.when(core == 0)
        def _():
            send(which, 4, 3, 2, beside).start()

        @pl.when(seq < 4)
        def _():
            outs[which][0] = jnp.zeros(outs[which].shape[1:], outs[which].dtype)

        @pl.when(seq < 3)
        def _():
            outs[which][1] = jnp.zeros(outs[which].shape[1:], outs[which].dtype)

        @pl.when(seq < 2)
        def _():
            outs[which][2] = jnp.zeros(outs[which].shape[1:], outs[which].dtype)

        @pl.when(seq < 1)
        def _():
            outs[which][3] = jnp.zeros(outs[which].shape[1:], outs[which].dtype)

    norm_rope(q_ref, q_out, q_gain_ref, cosine, sine)
    for which in range(2):

        @pl.when(seq >= 2)
        def _():
            send(which, 4, 2, 0, ahead).wait_recv()

            @pl.when(ahead < count)
            def _():
                send(which, 2, 0, 1, ahead).start()

            @pl.when(core == 0)
            def _():
                send(which, 2, 1, 3, beside).start()

            @pl.when(core == 1)
            def _():
                send(which, 2, 3, 2, beside).start()

    for which in range(2):

        @pl.when(seq >= 4)
        def _():
            send(which, 2, 0, 1, ahead).wait_recv()

            @pl.when(core == 1)
            def _():
                send(which, 0, 1, 3, beside).start()

    for which in range(2):

        @pl.when(seq >= 1)
        def _():
            send(which, 4, 3, 2, beside).wait_recv()

        @pl.when(seq >= 3)
        def _():
            send(which, 2, 1, 3, beside).wait_recv()

        @pl.when(ahead < count)
        def _():
            send(which, 4, 2, 0, ahead).wait_send()

            @pl.when(seq >= 2)
            def _():
                send(which, 2, 0, 1, ahead).wait_send()

        @pl.when((core == 0) | (seq >= 2))
        def _():
            send(which, 4, 3, 2, beside).wait_send()

        @pl.when(seq >= 2 + 2 * core)
        def _():
            send(which, 2, 1, 3, beside).wait_send()


def attention_kernel(
    q_ref, k_ref, v_ref, do_ref, dq_ref, gk_ref, gv_ref, gk_own_ref, gv_own_ref, ds_ref, w_ref
):
    rows, head_size = q_ref.shape
    span = k_ref.shape[0]
    scale = head_size ** (-0.5)
    head = lax.rem(pl.program_id(0), 2)
    first_pos = lax.axis_index("seq") * rows
    row = lax.broadcasted_iota(jnp.int32, (rows, span), 0)
    key = lax.broadcasted_iota(jnp.int32, (rows, span), 1)
    visible = (key > row) & (key <= row + WINDOW) & (key >= WINDOW - first_pos)
    across = (((1,), (1,)), ((), ()))
    scores = lax.dot_general(q_ref[...], k_ref[...], across, preferred_element_type=jnp.float32)
    scores = jnp.where(visible, scores * scale, MASKED)
    top = jnp.max(scores, axis=-1, keepdims=True)
    powers = jnp.exp(scores - top)
    weights = powers * (1.0 / jnp.sum(powers, axis=-1, keepdims=True))
    dweights = lax.dot_general(do_ref[...], v_ref[...], across, preferred_element_type=jnp.float32)
    delta = jnp.sum(weights * dweights, axis=-1, keepdims=True)
    dscores = (weights * (dweights - delta) * scale).astype(jnp.bfloat16)
    dq_ref[...] = jnp.dot(dscores, k_ref[...], preferred_element_type=jnp.float32)
    down = (((0,), (0,)), ((), ()))
    dk = lax.dot_general(dscores, q_ref[...], down, preferred_element_type=jnp.float32)
    dv = lax.dot_general(
        weights.astype(jnp.bfloat16), do_ref[...], down, preferred_element_type=jnp.float32
    )

    @pl.when(head == 0)
    def _():
        ds_ref[...] = dk
        w_ref[...] = dv

    @pl.when(head == 1)
    def _():
        dk_sum = ds_ref[...] + dk
        dv_sum = w_ref[...] + dv
        gk_ref[...] = dk_sum[:WINDOW].astype(jnp.bfloat16)
        gv_ref[...] = dv_sum[:WINDOW].astype(jnp.bfloat16)
        gk_own_ref[...] = dk_sum[WINDOW:]
        gv_own_ref[...] = dv_sum[WINDOW:]


def collect_kernel(
    count, gk_ref, gv_ref, gk_own_ref, gv_own_ref, q_ref, dq_ref, q_gain_ref, cos_ref, sin_ref,
    dk_out, dv_out, q_out, gain_out, beside_buf, behind_buf, sent_buf, send_sem, recv_sem,
):
    seq = lax.axis_index("seq")
    core = lax.rem(seq, 2)
    terms = (gk_ref, gv_ref)
    behind = seq - 2
    beside = other_core(seq)

    def swap(which, part):
        return pltpu.make_async_remote_copy(
            src_ref=terms[which].at[3 - 2 * part],
            dst_ref=beside_buf.at[which, part],
            send_sem=send_sem.at[which, part],
            recv_sem=recv_sem.at[which, part],
            device_id={"seq": beside},
            device_id_type=MESH,
        )

    def hop(which, part):
        return pltpu.make_async_remote_copy(
            src_ref=sent_buf.at[which, part],
            dst_ref=behind_buf.at[which, part],
            send_sem=send_sem.at[which, 2 + part],
            recv_sem=recv_sem.at[which, 2 + part],
            device_id={"seq": behind},
            device_id_type=MESH,
        )

    greet_neighbours(seq, count)
    for which in range(2):
        swap(which, 1).start()
        swap(which, 0).start()
    for which in range(2):
        swap(which, 1).wait()
        four = terms[which][0].astype(jnp.float32)

        @pl.when(core == 0)
        def _():
            sent_buf[which, 0] = terms[which][0]

        @pl.when(core == 1)
        def _():
            sent_buf[which, 0] = (four + beside_buf[which, 1].astype(jnp.float32)).astype(
                jnp.bfloat16
            )

        @pl.when(seq >= 2)
        def _():
            hop(which, 0).start()

    gain_grad = norm_rope_back(q_ref, dq_ref, q_out, q_gain_ref, cos_ref[...], sin_ref[...])
    half = gain_grad.shape[1] // 2
    gain_out[...] = jnp.zeros_like(gain_out)
    gain_out[0:1, :] = gain_grad[:, :half]
    gain_out[1:2, :] = gain_grad[:, half:]
    for which in range(2):
        swap(which, 0).wait()
        two = terms[which][2].astype(jnp.float32) + beside_buf[which, 1 - core].astype(jnp.float32)

        @pl.when(seq + 2 < count)
        def _():
            hop(which, 0).wait_recv()
            sent_buf[which, 1] = (two + behind_buf[which, 0].astype(jnp.float32)).astype(
                jnp.bfloat16
            )

        @pl.when(seq + 2 >= count)
        def _():
            sent_buf[which, 1] = two.astype(jnp.bfloat16)

        @pl.when(seq >= 2)
        def _():
            hop(which, 1).start()

    for which, (own_ref, out) in enumerate(((gk_own_ref, dk_out), (gv_own_ref, dv_out))):

        @pl.when(seq + 2 < count)
        def _():
            hop(which, 1).wait_recv()

        @pl.when(seq + 2 >= count)
        def _():
            behind_buf[which, 1] = jnp.zeros(behind_buf.shape[2:], behind_buf.dtype)

        total = own_ref[...] + behind_buf[which, 1].astype(jnp.float32)

        @pl.when(core == 0)
        def _():
            out[...] = (total + beside_buf[which, 0].astype(jnp.float32)).astype(out.dtype)

        @pl.when(core == 1)
        def _():
            out[...] = total.astype(out.dtype)

    for which in range(2):

        @pl.when(seq >= 2)
        def _():
            hop(which, 0).wait_send()
            hop(which, 1).wait_send()


def gain_sum_kernel(
    seq_size, dp_size, k_ref, dk_ref, gain_ref, k_gain_ref, cos_ref, sin_ref, k_out, o_ref,
    x_ref, slots_a, slots_b, slots_c, part_b, part_c, send_sem, recv_sem,
):
    seq = lax.axis_index("seq")
    dp = lax.axis_index("dp")
    z_lo_size = seq_size // LOW
    z_size = z_lo_size * (dp_size // X_SIZE)
    low = lax.rem(seq, LOW)
    z_lo = lax.div(seq, LOW)
    x_pos = lax.rem(dp, X_SIZE)
    z_pos = lax.div(dp, X_SIZE) * z_lo_size + z_lo

    def peer_a(k):
        return {"seq": z_lo * LOW + lax.rem(low + k, LOW), "dp": dp}

    def peer_b(k):
        return {"seq": seq, "dp": dp - x_pos + lax.rem(x_pos + k, X_SIZE)}

    def peer_c(k):
        z_other = lax.rem(z_pos + k, z_size)
        return {
            "seq": lax.rem(z_other, z_lo_size) * LOW + low,
            "dp": lax.div(z_other, z_lo_size) * X_SIZE + x_pos,
        }

    stages = ((LOW, peer_a, low), (X_SIZE, peer_b, x_pos), (z_size, peer_c, z_pos))
    barrier = pltpu.get_barrier_semaphore()
    total = 0
    for size, peer, _ in reversed(stages):
        for k in range(1, size):
            pl.semaphore_signal(barrier, inc=1, device_id=peer(k), device_id_type=MESH)
            total += 1
    gain_grad = norm_rope_back(k_ref, dk_ref, k_out, k_gain_ref, cos_ref[...], sin_ref[...])
    half = gain_grad.shape[1] // 2
    x_ref[...] = gain_ref[...]
    x_ref[2:3, :] = gain_grad[:, :half]
    x_ref[3:4, :] = gain_grad[:, half:]
    pl.semaphore_wait(barrier, total)

    base = 0
    sources = (x_ref, part_b, part_c)
    results = (part_b, part_c, o_ref)
    for (size, peer, mine), source, slots, result in zip(
        stages, sources, (slots_a, slots_b, slots_c), results
    ):
        copies = []
        for k in range(1, size):
            copy = pltpu.make_async_remote_copy(
                src_ref=source,
                dst_ref=slots.at[k],
                send_sem=send_sem.at[base + k - 1],
                recv_sem=recv_sem.at[base + k - 1],
                device_id=peer(k),
                device_id_type=MESH,
            )
            copy.start()
            copies.append(copy)
        slots[0] = source[...]
        for copy in copies:
            copy.wait()
        acc = slots[lax.rem(mine + size, size)]
        for j in range(1, size):
            acc = acc + slots[lax.rem(mine - j + size, size)]
        result[...] = acc
        base += size - 1


VMEM_SPEC = pl.BlockSpec(memory_space=pltpu.VMEM)


def halo(seq_size, *args):
    q, k = args[0], args[1]
    return pl.pallas_call(
        lambda *refs: halo_kernel(seq_size, *refs),
        out_shape=(
            jax.ShapeDtypeStruct(q.shape, jnp.bfloat16),
            jax.ShapeDtypeStruct((5,) + k.shape, jnp.bfloat16),
            jax.ShapeDtypeStruct((5,) + k.shape, jnp.bfloat16),
        ),
        in_specs=[VMEM_SPEC] * 7,
        out_specs=(VMEM_SPEC,) * 3,
        scratch_shapes=[
            pltpu.SemaphoreType.DMA((2, 4)),
            pltpu.SemaphoreType.DMA((2, 4)),
            pltpu.SemaphoreType.DMA,
        ],
        compiler_params=pltpu.CompilerParams(collective_id=1, has_side_effects=True),
        name="halo",
    )(*args)


def attention(q, keys, vals, grad_out, head_size):
    rows = q.shape[0]
    span = keys.shape[0]
    heads = q.shape[1] // head_size

    def by_head(height):
        return pl.BlockSpec((height, head_size), lambda h: (0, h))

    def by_group(height):
        return pl.BlockSpec((height, head_size), lambda h: (0, h // 2))

    def group_shape(height, dtype):
        return jax.ShapeDtypeStruct((height, keys.shape[1]), dtype)

    return pl.pallas_call(
        attention_kernel,
        grid=(heads,),
        out_shape=(
            jax.ShapeDtypeStruct(q.shape, jnp.float32),
            group_shape(WINDOW, jnp.bfloat16),
            group_shape(WINDOW, jnp.bfloat16),
            group_shape(rows, jnp.float32),
            group_shape(rows, jnp.float32),
        ),
        in_specs=[by_head(rows), by_group(span), by_group(span), by_head(rows)],
        out_specs=(by_head(rows), by_group(WINDOW), by_group(WINDOW), by_group(rows), by_group(rows)),
        scratch_shapes=[
            pltpu.VMEM((span, head_size), jnp.float32),
            pltpu.VMEM((span, head_size), jnp.float32),
        ],
        name="attention",
    )(q, keys, vals, grad_out)


def collect(seq_size, *args):
    own, q = args[2], args[4]
    rows, columns = own.shape
    return pl.pallas_call(
        lambda *refs: collect_kernel(seq_size, *refs),
        out_shape=(
            jax.ShapeDtypeStruct(own.shape, jnp.float32),
            jax.ShapeDtypeStruct(own.shape, jnp.bfloat16),
            jax.ShapeDtypeStruct(q.shape, jnp.bfloat16),
            jax.ShapeDtypeStruct((8, 128), jnp.float32),
        ),
        in_specs=[VMEM_SPEC] * 9,
        out_specs=(VMEM_SPEC,) * 4,
        scratch_shapes=[
            pltpu.VMEM((2, 2, rows, columns), jnp.bfloat16),
            pltpu.VMEM((2, 2, rows, columns), jnp.bfloat16),
            pltpu.VMEM((2, 2, rows, columns), jnp.bfloat16),
            pltpu.SemaphoreType.DMA((2, 4)),
            pltpu.SemaphoreType.DMA((2, 4)),
        ],
        compiler_params=pltpu.CompilerParams(collective_id=2, has_side_effects=True),
        name="collect",
    )(*args)


def gain_sum(seq_size, dp_size, *args):
    k, gains = args[0], args[2]
    z_size = seq_size // LOW * (dp_size // X_SIZE)
    peers = LOW + X_SIZE + z_size - 3
    return pl.pallas_call(
        lambda *refs: gain_sum_kernel(seq_size, dp_size, *refs),
        out_shape=(
            jax.ShapeDtypeStruct(k.shape, jnp.bfloat16),
            jax.ShapeDtypeStruct(gains.shape, jnp.float32),
        ),
        in_specs=[VMEM_SPEC] * 6,
        out_specs=(VMEM_SPEC,) * 2,
        scratch_shapes=[
            pltpu.VMEM(gains.shape, jnp.float32),
            pltpu.VMEM((LOW,) + gains.shape, jnp.float32),
            pltpu.VMEM((X_SIZE,) + gains.shape, jnp.float32),
            pltpu.VMEM((z_size,) + gains.shape, jnp.float32),
            pltpu.VMEM(gains.shape, jnp.float32),
            pltpu.VMEM(gains.shape, jnp.float32),
            pltpu.SemaphoreType.DMA((peers,)),
            pltpu.SemaphoreType.DMA((peers,)),
        ],
        compiler_params=pltpu.CompilerParams(collective_id=0, has_side_effects=True),
        name="gain_sum",
    )(*args)


def local(seq_size, dp_size, q_raw, k_raw, values, grad_out, q_gain, k_gain):
    q_local, k_local, v_local, do_local = q_raw[0], k_raw[0], values[0], grad_out[0]
    rows, columns = k_local.shape
    head_size = q_gain.shape[0]
    positions = lax.axis_index("seq") * rows + jnp.arange(rows, dtype=jnp.int32)
    cosine, sine = rope_tables(positions, head_size)
    q_gain, k_gain = q_gain[None], k_gain[None]
    q_rot, keys, vals = halo(seq_size, q_local, k_local, v_local, q_gain, k_gain, cosine, sine)
    dq_rot, gk, gv, gk_own, gv_own = attention(
        q_rot, keys.reshape(5 * rows, columns), vals.reshape(5 * rows, columns), do_local, head_size
    )
    dk_rot, grad_v, grad_q, gains = collect(
        seq_size, gk.reshape(4, rows, columns), gv.reshape(4, rows, columns), gk_own, gv_own,
        q_local, dq_rot, q_gain, cosine, sine,
    )
    grad_k, gains = gain_sum(seq_size, dp_size, k_local, dk_rot, gains, k_gain, cosine, sine)
    gains = gains[:4].reshape(2, head_size)
    return (grad_q[None], grad_k[None], grad_v[None], gains[0], gains[1])


def solution(mesh):
    return jax.shard_map(
        lambda *args: local(mesh.shape["seq"], mesh.shape["dp"], *args),
        mesh=mesh,
        in_specs=(
            P("dp", "seq", None),
            P("dp", "seq", None),
            P("dp", "seq", None),
            P("dp", "seq", None),
            P(),
            P(),
        ),
        out_specs=(P("dp", "seq", None), P("dp", "seq", None), P("dp", "seq", None), P(), P()),
        check_vma=False,
    )
```

time: 184 us -> 112 us (0.61)
  Pallas kernels: 37 us -> 105 us
  starting transfers between devices: 40.1 us -> 0 us
  matrix products: 34.1 us -> 0 us
  local copies, waits for them, and re-layouts: 33.5 us -> 4.49 us
  other arithmetic: 24.9 us -> 1.25 us
  waiting for transfers between devices: 11.8 us -> 0 us
    pallas_call x0 -> x3, Pallas kernels: none -> 72.8 us  [the longest x1 40.5 us: collect(): pl.pallas_call(lambda *refs: collect_kernel(seq_size, *refs), out_shape=(...]
    ppermute x16 -> x0, starting transfers between devices: 40.1 us -> none  [the longest x8 20.6 us: core_swap(): return lax.ppermute(array, 'seq', [(i, i ^ 1) for i in range(count)])]
    dot_general x5 -> x0, matrix products: 34.1 us -> none  [the longest x1 11.8 us: local(): jnp.einsum('kgts,tkgd->skd', dscores, q_heads, preferred_element_type=jnp...]
    ppermute x16 -> x0, waiting for transfers between devices: 11.8 us -> none  [the longest x8 11.8 us: from_behind(): return lax.ppermute(array, 'seq', pairs)]
    unnamed x39 -> x7, local copies, waits for them, and re-layouts: 13 us -> 3.17 us
    convert_element_type x7 -> x0, other arithmetic: 8.58 us -> none  [the longest x2 3.09 us: collect(): from_four = from_behind(four.astype(jnp.bfloat16), -2).astype(jnp.float32)]
    concatenate x8 -> x0, local copies, waits for them, and re-layouts: 8.19 us -> none  [the longest x7 7.33 us: halo(): return jnp.concatenate([four, three, two, one, own], axis=0)]
    select_n x3 -> x0, other arithmetic: 5.41 us -> none  [the longest x2 3.59 us: halo(): one = core_swap(jnp.where(first_core, own, two))]
  transfers between devices with their start and end apart: 16 -> 0, of which waited for: 4 -> 0; matrix products, arithmetic and copies ran while one was open for 25% -> 0% of each run, Pallas kernels for 0% -> 0%
where the time goes in v2:
time: 112 us; the launch traced here: 111 us
  Pallas kernels  105 us (94%)
  local copies, waits for them, and re-layouts  4.49 us (4%)
  other arithmetic  1.25 us (1%)
    pallas_call x1, Pallas kernels, collect(): pl.pallas_call(lambda *refs: collect_kernel(seq_size, *refs), out_shape=(...  40.5 us
    pallas_call x1, Pallas kernels, gain_sum(): pl.pallas_call(lambda *refs: gain_sum_kernel(seq_size, dp_size, *refs), o...  32 us
    pallas_call x1, Pallas kernels, halo(): pl.pallas_call(lambda *refs: halo_kernel(seq_size, *refs), out_shape=(jax...  22.2 us
    pallas_call x1, Pallas kernels, attention(): pl.pallas_call(attention_kernel, grid=(heads,), out_shape=(jax.ShapeDtype...  10 us
    unnamed x7, local copies, waits for them, and re-layouts  3.17 us

profile of v2, /device:TPU:1, one launch (start us, length us, event | category | flops | bytes accessed | tf_op | source)
XLA Modules:
  0.0 111.2 jit_solution(9731851293187453455)
XLA Ops:
  0.7 1.2 %multiply_sine_fusion = (f32[256,128]{1,0:T(8,128)}, f32[256,128]{1,0:T(8,128)}) fusion(f32[128]{0:T(128)S(1)} %multiply_power_fusion, f32[256]{0:T(256)S(1)} %add_convert_fusion), kind=kLoop, calls=%fused_computation | loop fusion | flops 32768 | bytes 263680 | tf_op jit(solution)/shard_map/sin | solution.py:24
  1.9 22.2 %halo.1 = (bf16[256,1024]{1,0:T(8,128)(2,1)}, bf16[5,256,512]{2,1,0:T(8,128)(2,1)}, bf16[5,256,512]{2,1,0:T(8,128)(2,1)}) custom-call(bf16[256,1024]{1,0:T(8,128)(2,1)} %bitcast.17, bf16[256,512]{1,0:T(8,128)(2,1)} %bitcast.21, bf16[256,512]{1,0:T(8,128)(2,1)} %bitcast.27, f32[1,256]{1,0:T(1,128)} %bitcast.32, f32[1,256]{1,0:T(1,128)} %bitcast.30, ...), custom_call_target="tpu_custom_call" | custom-call | tf_op jit(solution)/shard_map/halo/pallas_call | solution.py:420
  24.1 10.0 %attention.1 = (f32[256,1024]{1,0:T(8,128)}, bf16[1024,512]{1,0:T(8,128)(2,1)}, bf16[1024,512]{1,0:T(8,128)(2,1)}, f32[256,512]{1,0:T(8,128)}, f32[256,512]{1,0:T(8,128)}) custom-call(bf16[256,1024]{1,0:T(8,128)(2,1)} %get-tuple-element.19.q_ref, bf16[1280,512]{1,0:T(8,128)(2,1)} %bitcast.19, bf16[1280,512]{1,0:T(8,128)(2,1)} %bitcast.20, ...), custom_call_target="tpu_custom_call" | custom-call | tf_op jit(solution)/shard_map/attention/pallas_call | solution.py:453
  34.2 40.5 %collect.1 = (f32[256,512]{1,0:T(8,128)}, bf16[256,512]{1,0:T(8,128)(2,1)}, bf16[256,1024]{1,0:T(8,128)(2,1)}, f32[8,128]{1,0:T(8,128)}) custom-call(bf16[4,256,512]{2,1,0:T(8,128)(2,1)} %bitcast.23, bf16[4,256,512]{2,1,0:T(8,128)(2,1)} %bitcast.24, f32[256,512]{1,0:T(8,128)} %get-tuple-element.24.refs_2_, f32[256,512]{1,0:T(8,128)} %get-tuple-element.25.refs_3_, ...), custom_call_target="tpu_custom_call" | custom-call | tf_op jit(solution)/shard_map/collect/pallas_call | solution.py:476
  74.7 0.0 copy-start
  74.7 0.0 copy-start.1
  74.7 32.0 %gain_sum.1 = (bf16[256,512]{1,0:T(8,128)(2,1)}, f32[8,128]{1,0:T(8,128)}) custom-call(bf16[256,512]{1,0:T(8,128)(2,1)} %bitcast.22, f32[256,512]{1,0:T(8,128)} %get-tuple-element.28.refs_1_, f32[8,128]{1,0:T(8,128)} %get-tuple-element.29.refs_2_, f32[1,256]{1,0:T(1,128)} %bitcast.31, f32[256,128]{1,0:T(8,128)} %get-tuple-element.36.refs_5_.refs_7_.refs_4_, ...), custom_call_target="tpu_custom_call" | custom-call | tf_op jit(solution)/shard_map/gain_sum/pallas_call | solution.py:502
  106.7 1.3 %slice_bitcast_fusion = (f32[256]{0:T(256)}, f32[256]{0:T(256)}) fusion(f32[8,128]{1,0:T(8,128)} %get-tuple-element.32), kind=kLoop, calls=%fused_computation.2 | loop fusion | bytes 4096 | tf_op jit(solution)/shard_map/squeeze | solution.py:542
  108.1 0.0 copy-done
  108.1 0.8 copy.14
  108.9 1.7 %copy.15 = bf16[1,256,512]{2,1,0:T(8,128)(2,1)} copy(bf16[1,256,512]{2,1,0:T(8,128)(2,1)} %bitcast.29) | data formatting | bytes 524288
  110.5 0.0 copy-done.1
  110.5 0.7 copy.16
  (2 shorter events, 0.0 us)
Async XLA Ops:
  74.7 33.4 %copy-start = (bf16[256,1024]{1,0:T(8,128)(2,1)S(1)}, bf16[256,1024]{1,0:T(8,128)(2,1)}, u32[]{:S(2)}) copy-start(bf16[256,1024]{1,0:T(8,128)(2,1)} %get-tuple-element.27) | copy-start | bytes 1572868
  74.7 35.8 %copy-start.1 = (bf16[256,512]{1,0:T(8,128)(2,1)S(1)}, bf16[256,512]{1,0:T(8,128)(2,1)}, u32[]{:S(2)}) copy-start(bf16[256,512]{1,0:T(8,128)(2,1)} %get-tuple-element.31) | copy-start | bytes 786436

commit v3 on v2

v3 whole, which is shorter than its diff:
```python
import jax
import jax.numpy as jnp
from jax import lax
from jax.experimental import pallas as pl
from jax.experimental.pallas import tpu as pltpu
from jax.sharding import PartitionSpec as P

WINDOW = 1024


EPS = 1e-06
ROPE_BASE = 10000.0
MASKED = -1e30
MESH = pl.DeviceIdType.MESH

LOW = 8
X_SIZE = 4


def rope_tables(positions, head_size):
    half_size = head_size // 2
    freqs = jnp.power(ROPE_BASE, -(2.0 * jnp.arange(half_size, dtype=jnp.float32)) / head_size)
    angles = positions.astype(jnp.float32)[:, None] * freqs[None, :]
    return (jnp.cos(angles), jnp.sin(angles))


def norm_rope(raw_ref, out_ref, gain_ref, cosine, sine):
    head_size = gain_ref.shape[1]
    half = head_size // 2
    for start in range(0, raw_ref.shape[1], head_size):
        x = raw_ref[:, start : start + head_size].astype(jnp.float32)
        scaled = x * lax.rsqrt(jnp.mean(x * x, axis=-1, keepdims=True) + EPS) * gain_ref[...]
        lower, upper = scaled[:, :half], scaled[:, half:]
        out_ref[:, start : start + half] = (lower * cosine - upper * sine).astype(out_ref.dtype)
        out_ref[:, start + half : start + head_size] = (upper * cosine + lower * sine).astype(
            out_ref.dtype
        )


def norm_rope_back(raw_ref, grad_ref, out_ref, gain_ref, cosine, sine):
    head_size = gain_ref.shape[1]
    half = head_size // 2
    gain_grad = jnp.zeros((1, head_size), jnp.float32)
    for start in range(0, raw_ref.shape[1], head_size):
        x = raw_ref[:, start : start + head_size].astype(jnp.float32)
        inverse = lax.rsqrt(jnp.mean(x * x, axis=-1, keepdims=True) + EPS)
        normed = x * inverse
        lower = grad_ref[:, start : start + half]
        upper = grad_ref[:, start + half : start + head_size]
        d_scaled = jnp.concatenate(
            [lower * cosine + upper * sine, upper * cosine - lower * sine], axis=-1
        )
        gain_grad = gain_grad + jnp.sum(d_scaled * normed, axis=0, keepdims=True)
        d_normed = d_scaled * gain_ref[...]
        along = jnp.mean(d_normed * normed, axis=-1, keepdims=True)
        out_ref[:, start : start + head_size] = (inverse * (d_normed - normed * along)).astype(
            out_ref.dtype
        )
    return gain_grad


def greet_signals(barrier, seq, count):
    pl.semaphore_signal(barrier, inc=1, device_id={"seq": other_core(seq)}, device_id_type=MESH)

    @pl.when(seq >= 2)
    def _():
        pl.semaphore_signal(barrier, inc=1, device_id={"seq": seq - 2}, device_id_type=MESH)

    @pl.when(seq + 2 < count)
    def _():
        pl.semaphore_signal(barrier, inc=1, device_id={"seq": seq + 2}, device_id_type=MESH)


def greet_waits(barrier, seq, count, others):
    inside = (seq >= 2) & (seq + 2 < count)

    @pl.when(inside)
    def _():
        pl.semaphore_wait(barrier, others + 3)

    @pl.when(jnp.logical_not(inside))
    def _():
        pl.semaphore_wait(barrier, others + 2)


def other_core(seq):
    return seq + 1 - 2 * lax.rem(seq, 2)


def halo_kernel(
    count, q_ref, k_ref, v_ref, q_gain_ref, k_gain_ref, cos_ref, sin_ref,
    q_out, k_out, v_out, send_sem, recv_sem, copy_sem,
):
    seq = lax.axis_index("seq")
    core = lax.rem(seq, 2)
    cosine, sine = cos_ref[...], sin_ref[...]
    outs = (v_out, k_out)

    def send(which, source, target, hop, device):
        return pltpu.make_async_remote_copy(
            src_ref=outs[which].at[source],
            dst_ref=outs[which].at[target],
            send_sem=send_sem.at[which, hop],
            recv_sem=recv_sem.at[which, hop],
            device_id={"seq": device},
            device_id_type=MESH,
        )

    ahead = seq + 2
    beside = other_core(seq)
    local = pltpu.make_async_copy(v_ref, v_out.at[4], copy_sem)
    local.start()
    barrier = pltpu.get_barrier_semaphore()
    greet_signals(barrier, seq, count)
    greet_waits(barrier, seq, count, 0)
    local.wait()

    def send_own(which):
        @pl.when(ahead < count)
        def _():
            send(which, 4, 2, 0, ahead).start()

    send_own(0)
    norm_rope(k_ref, k_out.at[4], k_gain_ref, cosine, sine)
    send_own(1)
    for which in range(2):

        @pl.when(core == 0)
        def _():
            send(which, 4, 3, 2, beside).start()

        @pl.when(seq < 4)
        def _():
            outs[which][0] = jnp.zeros(outs[which].shape[1:], outs[which].dtype)

        @pl.when(seq < 3)
        def _():
            outs[which][1] = jnp.zeros(outs[which].shape[1:], outs[which].dtype)

        @pl.when(seq < 2)
        def _():
            outs[which][2] = jnp.zeros(outs[which].shape[1:], outs[which].dtype)

        @pl.when(seq < 1)
        def _():
            outs[which][3] = jnp.zeros(outs[which].shape[1:], outs[which].dtype)

    norm_rope(q_ref, q_out, q_gain_ref, cosine, sine)
    for which in range(2):

        @pl.when(seq >= 2)
        def _():
            send(which, 4, 2, 0, ahead).wait_recv()

            @pl.when(ahead < count)
            def _():
                send(which, 2, 0, 1, ahead).start()

            @pl.when(core == 0)
            def _():
                send(which, 2, 1, 3, beside).start()

            @pl.when(core == 1)
            def _():
                send(which, 2, 3, 2, beside).start()

    for which in range(2):

        @pl.when(seq >= 4)
        def _():
            send(which, 2, 0, 1, ahead).wait_recv()

            @pl.when(core == 1)
            def _():
                send(which, 0, 1, 3, beside).start()

    for which in range(2):

        @pl.when(seq >= 1)
        def _():
            send(which, 4, 3, 2, beside).wait_recv()

        @pl.when(seq >= 3)
        def _():
            send(which, 2, 1, 3, beside).wait_recv()

        @pl.when(ahead < count)
        def _():
            send(which, 4, 2, 0, ahead).wait_send()

            @pl.when(seq >= 2)
            def _():
                send(which, 2, 0, 1, ahead).wait_send()

        @pl.when((core == 0) | (seq >= 2))
        def _():
            send(which, 4, 3, 2, beside).wait_send()

        @pl.when(seq >= 2 + 2 * core)
        def _():
            send(which, 2, 1, 3, beside).wait_send()


def attention_group(group, q_ref, keys_ref, vals_ref, do_ref, dq_ref, terms, owns):
    count, rows, columns = keys_ref.shape
    head_size = columns // 2
    span = count * rows
    scale = head_size ** (-0.5)
    lanes = slice(group * head_size, (group + 1) * head_size)
    first_pos = lax.axis_index("seq") * rows
    row = lax.broadcasted_iota(jnp.int32, (rows, span), 0)
    key = lax.broadcasted_iota(jnp.int32, (rows, span), 1)
    visible = (key > row) & (key <= row + WINDOW) & (key >= WINDOW - first_pos)
    across = (((1,), (1,)), ((), ()))
    down = (((0,), (0,)), ((), ()))
    keys = keys_ref[:, :, lanes].reshape(span, head_size)
    vals = vals_ref[:, :, lanes].reshape(span, head_size)
    sums = None
    for head in (2 * group, 2 * group + 1):
        cols = slice(head * head_size, (head + 1) * head_size)
        q, do = q_ref[:, cols], do_ref[:, cols]
        scores = lax.dot_general(q, keys, across, preferred_element_type=jnp.float32)
        scores = jnp.where(visible, scores * scale, MASKED)
        top = jnp.max(scores, axis=-1, keepdims=True)
        powers = jnp.exp(scores - top)
        weights = powers * (1.0 / jnp.sum(powers, axis=-1, keepdims=True))
        dweights = lax.dot_general(do, vals, across, preferred_element_type=jnp.float32)
        delta = jnp.sum(weights * dweights, axis=-1, keepdims=True)
        dscores = (weights * (dweights - delta) * scale).astype(jnp.bfloat16)
        dq_ref[:, cols] = jnp.dot(dscores, keys, preferred_element_type=jnp.float32)
        grads = (
            lax.dot_general(dscores, q, down, preferred_element_type=jnp.float32),
            lax.dot_general(
                weights.astype(jnp.bfloat16), do, down, preferred_element_type=jnp.float32
            ),
        )
        sums = grads if sums is None else tuple(x + y for x, y in zip(sums, grads))
    for which in range(2):
        behind = sums[which][:WINDOW].reshape(count - 1, rows, head_size)
        terms[which, :, :, lanes] = behind.astype(jnp.bfloat16)
        owns[which, :, lanes] = sums[which][WINDOW:]


def key_gain_grad(keys_ref, terms, owns, cosine, sine, turn_ref, gain_ref):
    count, rows, columns = keys_ref.shape
    head_size = columns // 2
    half = head_size // 2
    twice_cos = cosine * cosine - sine * sine
    twice_sin = 2.0 * cosine * sine
    same = jnp.zeros((1, half), jnp.float32)
    turned = jnp.zeros((1, half), jnp.float32)
    for block in range(count):
        real = jnp.zeros((1, half), jnp.float32)
        imag = jnp.zeros((1, half), jnp.float32)
        for start in (0, head_size):
            lower, upper = slice(start, start + half), slice(start + half, start + head_size)
            if block < count - 1:
                a_low = terms[0, block, :, lower].astype(jnp.float32)
                a_up = terms[0, block, :, upper].astype(jnp.float32)
            else:
                a_low, a_up = owns[0, :, lower], owns[0, :, upper]
            b_low = keys_ref[block, :, lower].astype(jnp.float32)
            b_up = keys_ref[block, :, upper].astype(jnp.float32)
            low, up = a_low * b_low, a_up * b_up
            x, y = low - up, a_low * b_up + a_up * b_low
            same = same + jnp.sum(low + up, axis=0, keepdims=True)
            real = real + jnp.sum(x * twice_cos + y * twice_sin, axis=0, keepdims=True)
            imag = imag + jnp.sum(y * twice_cos - x * twice_sin, axis=0, keepdims=True)
        turned = (
            turned
            + real * turn_ref[block : block + 1, :half]
            - imag * turn_ref[block : block + 1, half:]
        )
    grad = jnp.concatenate([same + turned, same - turned], axis=-1) * 0.5
    return grad / gain_ref[...]


def backward_kernel(
    seq_size, dp_size, q_rot_ref, keys_ref, vals_ref, do_ref, q_ref, k_ref, q_gain_ref, k_gain_ref,
    cos_ref, sin_ref, turn_ref, q_out, k_out, v_out, q_gain_out, k_gain_out,
    dq_ref, terms, owns, beside_buf, behind_buf, sent_buf, send_sem, recv_sem,
    x_ref, slots_a, slots_b, slots_c, part_b, part_c, gain_send_sem, gain_recv_sem,
):
    seq = lax.axis_index("seq")
    dp = lax.axis_index("dp")
    core = lax.rem(seq, 2)
    behind = seq - 2
    beside = other_core(seq)
    cosine, sine = cos_ref[...], sin_ref[...]

    z_lo_size = seq_size // LOW
    z_size = z_lo_size * (dp_size // X_SIZE)
    low = lax.rem(seq, LOW)
    z_lo = lax.div(seq, LOW)
    x_pos = lax.rem(dp, X_SIZE)
    z_pos = lax.div(dp, X_SIZE) * z_lo_size + z_lo

    def peer_a(k):
        return {"seq": z_lo * LOW + lax.rem(low + k, LOW), "dp": dp}

    def peer_b(k):
        return {"seq": seq, "dp": dp - x_pos + lax.rem(x_pos + k, X_SIZE)}

    def peer_c(k):
        z_other = lax.rem(z_pos + k, z_size)
        return {
            "seq": lax.rem(z_other, z_lo_size) * LOW + low,
            "dp": lax.div(z_other, z_lo_size) * X_SIZE + x_pos,
        }

    stages = ((LOW, peer_a, low), (X_SIZE, peer_b, x_pos), (z_size, peer_c, z_pos))
    barrier = pltpu.get_barrier_semaphore()
    greeted = 0
    for size, peer, _ in reversed(stages):
        for k in range(1, size):
            pl.semaphore_signal(barrier, inc=1, device_id=peer(k), device_id_type=MESH)
            greeted += 1
    greet_signals(barrier, seq, seq_size)
    heads = (q_rot_ref, keys_ref, vals_ref, do_ref, dq_ref, terms, owns)
    attention_group(0, *heads)
    attention_group(1, *heads)
    greet_waits(barrier, seq, seq_size, greeted)

    def swap(which, part):
        return pltpu.make_async_remote_copy(
            src_ref=terms.at[which, 3 - 2 * part],
            dst_ref=beside_buf.at[which, part],
            send_sem=send_sem.at[which, part],
            recv_sem=recv_sem.at[which, part],
            device_id={"seq": beside},
            device_id_type=MESH,
        )

    def hop(which, part):
        return pltpu.make_async_remote_copy(
            src_ref=sent_buf.at[which, part],
            dst_ref=behind_buf.at[which, part],
            send_sem=send_sem.at[which, 2 + part],
            recv_sem=recv_sem.at[which, 2 + part],
            device_id={"seq": behind},
            device_id_type=MESH,
        )

    sources = (x_ref, part_b, part_c)
    results = (part_b, part_c, x_ref)
    slot_refs = (slots_a, slots_b, slots_c)
    bases = (0, LOW - 1, LOW + X_SIZE - 2)

    def gain_copies(stage):
        size, peer, _ = stages[stage]
        return [
            pltpu.make_async_remote_copy(
                src_ref=sources[stage],
                dst_ref=slot_refs[stage].at[k],
                send_sem=gain_send_sem.at[bases[stage] + k - 1],
                recv_sem=gain_recv_sem.at[bases[stage] + k - 1],
                device_id=peer(k),
                device_id_type=MESH,
            )
            for k in range(1, size)
        ]

    def gain_start(stage):
        for copy in gain_copies(stage):
            copy.start()
        slot_refs[stage][0] = sources[stage][...]

    def gain_end(stage):
        for copy in gain_copies(stage):
            copy.wait()
        size, _, mine = stages[stage]
        slots = slot_refs[stage]
        acc = slots[lax.rem(mine + size, size)]
        for j in range(1, size):
            acc = acc + slots[lax.rem(mine - j + size, size)]
        results[stage][...] = acc

    for which in range(2):
        swap(which, 1).start()
    for which in range(2):
        swap(which, 0).start()
    for which in range(2):
        swap(which, 1).wait()
        four = terms[which, 0]

        @pl.when(core == 0)
        def _():
            sent_buf[which, 0] = four

        @pl.when(core == 1)
        def _():
            sent_buf[which, 0] = (
                four.astype(jnp.float32) + beside_buf[which, 1].astype(jnp.float32)
            ).astype(jnp.bfloat16)

        @pl.when(seq >= 2)
        def _():
            hop(which, 0).start()

    k_gain = key_gain_grad(keys_ref, terms, owns, cosine, sine, turn_ref, k_gain_ref)
    q_gain = norm_rope_back(q_ref, dq_ref, q_out, q_gain_ref, cosine, sine)
    half = q_gain.shape[1] // 2
    x_ref[...] = jnp.zeros_like(x_ref)
    x_ref[0:1, :] = q_gain[:, :half]
    x_ref[1:2, :] = q_gain[:, half:]
    x_ref[2:3, :] = k_gain[:, :half]
    x_ref[3:4, :] = k_gain[:, half:]
    gain_start(0)
    for which in range(2):
        swap(which, 0).wait()
        two = terms[which, 2].astype(jnp.float32) + beside_buf[which, 1 - core].astype(jnp.float32)

        @pl.when(seq + 2 < seq_size)
        def _():
            hop(which, 0).wait_recv()
            sent_buf[which, 1] = (two + behind_buf[which, 0].astype(jnp.float32)).astype(
                jnp.bfloat16
            )

        @pl.when(seq + 2 >= seq_size)
        def _():
            sent_buf[which, 1] = two.astype(jnp.bfloat16)

        @pl.when(seq >= 2)
        def _():
            hop(which, 1).start()

        gain_end(which)
        gain_start(which + 1)

    for which in range(2):

        @pl.when(seq + 2 < seq_size)
        def _():
            hop(which, 1).wait_recv()
            owns[which] = owns[which] + behind_buf[which, 1].astype(jnp.float32)

        @pl.when(core == 0)
        def _():
            owns[which] = owns[which] + beside_buf[which, 0].astype(jnp.float32)

        if which == 0:
            norm_rope_back(k_ref, owns.at[0], k_out, k_gain_ref, cosine, sine)

    v_out[...] = owns[1].astype(v_out.dtype)
    gain_end(2)
    for out, start in ((q_gain_out, 0), (k_gain_out, 2)):
        out[:, :half] = x_ref[start : start + 1, :]
        out[:, half:] = x_ref[start + 1 : start + 2, :]
    for which in range(2):

        @pl.when(seq >= 2)
        def _():
            hop(which, 0).wait_send()
            hop(which, 1).wait_send()


VMEM_SPEC = pl.BlockSpec(memory_space=pltpu.VMEM)


def halo(seq_size, *args):
    q, k = args[0], args[1]
    return pl.pallas_call(
        lambda *refs: halo_kernel(seq_size, *refs),
        out_shape=(
            jax.ShapeDtypeStruct(q.shape, jnp.bfloat16),
            jax.ShapeDtypeStruct((5,) + k.shape, jnp.bfloat16),
            jax.ShapeDtypeStruct((5,) + k.shape, jnp.bfloat16),
        ),
        in_specs=[VMEM_SPEC] * 7,
        out_specs=(VMEM_SPEC,) * 3,
        scratch_shapes=[
            pltpu.SemaphoreType.DMA((2, 4)),
            pltpu.SemaphoreType.DMA((2, 4)),
            pltpu.SemaphoreType.DMA,
        ],
        compiler_params=pltpu.CompilerParams(collective_id=1, has_side_effects=True),
        name="halo",
    )(*args)


def backward(seq_size, dp_size, *args):
    q, keys, k = args[0], args[1], args[5]
    rows, columns = k.shape
    head_size = columns // 2
    z_size = seq_size // LOW * (dp_size // X_SIZE)
    peers = LOW + X_SIZE + z_size - 3
    gains = (8, 128)
    return pl.pallas_call(
        lambda *refs: backward_kernel(seq_size, dp_size, *refs),
        out_shape=(
            jax.ShapeDtypeStruct(q.shape, jnp.bfloat16),
            jax.ShapeDtypeStruct(k.shape, jnp.bfloat16),
            jax.ShapeDtypeStruct(k.shape, jnp.bfloat16),
            jax.ShapeDtypeStruct((1, head_size), jnp.float32),
            jax.ShapeDtypeStruct((1, head_size), jnp.float32),
        ),
        in_specs=[VMEM_SPEC] * 11,
        out_specs=(VMEM_SPEC,) * 5,
        scratch_shapes=[
            pltpu.VMEM(q.shape, jnp.float32),
            pltpu.VMEM((2, keys.shape[0] - 1, rows, columns), jnp.bfloat16),
            pltpu.VMEM((2, rows, columns), jnp.float32),
            pltpu.VMEM((2, 2, rows, columns), jnp.bfloat16),
            pltpu.VMEM((2, 2, rows, columns), jnp.bfloat16),
            pltpu.VMEM((2, 2, rows, columns), jnp.bfloat16),
            pltpu.SemaphoreType.DMA((2, 4)),
            pltpu.SemaphoreType.DMA((2, 4)),
            pltpu.VMEM(gains, jnp.float32),
            pltpu.VMEM((LOW,) + gains, jnp.float32),
            pltpu.VMEM((X_SIZE,) + gains, jnp.float32),
            pltpu.VMEM((z_size,) + gains, jnp.float32),
            pltpu.VMEM(gains, jnp.float32),
            pltpu.VMEM(gains, jnp.float32),
            pltpu.SemaphoreType.DMA((peers,)),
            pltpu.SemaphoreType.DMA((peers,)),
        ],
        compiler_params=pltpu.CompilerParams(collective_id=0, has_side_effects=True),
        name="backward",
    )(*args)


def local(seq_size, dp_size, q_raw, k_raw, values, grad_out, q_gain, k_gain):
    q_local, k_local, v_local, do_local = q_raw[0], k_raw[0], values[0], grad_out[0]
    rows = k_local.shape[0]
    head_size = q_gain.shape[0]
    positions = lax.axis_index("seq") * rows + jnp.arange(rows, dtype=jnp.int32)
    cosine, sine = rope_tables(positions, head_size)
    back = jnp.maximum(4 - jnp.arange(8, dtype=jnp.int32), 0) * (2 * rows)
    turn = jnp.concatenate(rope_tables(back, head_size), axis=-1)
    q_gain, k_gain = q_gain[None], k_gain[None]
    q_rot, keys, vals = halo(seq_size, q_local, k_local, v_local, q_gain, k_gain, cosine, sine)
    grad_q, grad_k, grad_v, grad_q_gain, grad_k_gain = backward(
        seq_size, dp_size, q_rot, keys, vals, do_local, q_local, k_local, q_gain, k_gain,
        cosine, sine, turn,
    )
    return (grad_q[None], grad_k[None], grad_v[None], grad_q_gain[0], grad_k_gain[0])


def solution(mesh):
    return jax.shard_map(
        lambda *args: local(mesh.shape["seq"], mesh.shape["dp"], *args),
        mesh=mesh,
        in_specs=(
            P("dp", "seq", None),
            P("dp", "seq", None),
            P("dp", "seq", None),
            P("dp", "seq", None),
            P(),
            P(),
        ),
        out_specs=(P("dp", "seq", None), P("dp", "seq", None), P("dp", "seq", None), P(), P()),
        check_vma=False,
    )
```

time: 112 us -> 92.6 us (0.83)
  the two profiles are of different devices: /device:TPU:1 before, /device:TPU:25 now
where the time goes in v3:
time: 92.6 us; the launch traced here: 92.4 us
  Pallas kernels  84.3 us (91%)
  local copies, waits for them, and re-layouts  5.42 us (6%)
  other arithmetic  1.97 us (2%)
    pallas_call x1, Pallas kernels, backward(): pl.pallas_call(lambda *refs: backward_kernel(seq_size, dp_size, *refs), o...  55.3 us
    pallas_call x1, Pallas kernels, halo(): pl.pallas_call(lambda *refs: halo_kernel(seq_size, *refs), out_shape=(jax...  29 us
    unnamed x11, local copies, waits for them, and re-layouts  5.42 us

profile of v3, /device:TPU:25, one launch (start us, length us, event | category | flops | bytes accessed | tf_op | source)
XLA Modules:
  0.0 92.4 jit_solution(18020371271206398667)
XLA Ops:
  0.7 0.1 multiply_cosine_fusion.1
  0.8 0.6 pad_maximum_fusion.refs_10_
  1.4 1.2 %multiply_sine_fusion = (f32[256,128]{1,0:T(8,128)}, f32[256,128]{1,0:T(8,128)}) fusion(f32[128]{0:T(128)S(1)} %multiply_power_fusion, f32[256]{0:T(256)S(1)} %add_convert_fusion), kind=kLoop, calls=%fused_computation | loop fusion | flops 32768 | bytes 263680 | tf_op jit(solution)/shard_map/sin | solution.py:24
  2.6 29.0 %halo.1 = (bf16[256,1024]{1,0:T(8,128)(2,1)}, bf16[5,256,512]{2,1,0:T(8,128)(2,1)}, bf16[5,256,512]{2,1,0:T(8,128)(2,1)}) custom-call(bf16[256,1024]{1,0:T(8,128)(2,1)} %bitcast.11, bf16[256,512]{1,0:T(8,128)(2,1)} %bitcast.13, bf16[256,512]{1,0:T(8,128)(2,1)} %bitcast.17, f32[1,256]{1,0:T(1,128)} %bitcast.20, f32[1,256]{1,0:T(1,128)} %bitcast.22, ...), custom_call_target="tpu_custom_call" | custom-call | tf_op jit(solution)/shard_map/halo/pallas_call | solution.py:463
  31.7 55.3 %backward.1 = (bf16[256,1024]{1,0:T(8,128)(2,1)}, bf16[256,512]{1,0:T(8,128)(2,1)}, bf16[256,512]{1,0:T(8,128)(2,1)}, f32[1,256]{1,0:T(1,128)}, f32[1,256]{1,0:T(1,128)}) custom-call(bf16[256,1024]{1,0:T(8,128)(2,1)} %get-tuple-element.13.refs_0_, bf16[5,256,512]{2,1,0:T(8,128)(2,1)} %get-tuple-element.14.refs_1_, ...), custom_call_target="tpu_custom_call" | custom-call | tf_op jit(solution)/shard_map/backward/pallas_call | solution.py:489
  87.0 0.0 copy-start
  87.0 0.0 copy-start.2
  87.0 0.0 copy-start.1
  87.0 1.9 %copy.16 = bf16[1,256,1024]{2,1,0:T(8,128)(2,1)} copy(bf16[1,256,1024]{2,1,0:T(8,128)(2,1)} %bitcast.16) | data formatting | bytes 1048576
  88.9 1.7 %copy.17 = bf16[1,256,512]{2,1,0:T(8,128)(2,1)} copy(bf16[1,256,512]{2,1,0:T(8,128)(2,1)} %bitcast.19) | data formatting | bytes 524288
  90.6 0.0 copy-done
  90.6 0.7 copy.18
  91.3 0.0 copy-done.2
  91.3 0.6 copy.19
  91.8 0.0 copy-done.1
  91.8 0.6 copy.20
  (3 shorter events, 0.0 us)
Async XLA Ops:
  87.0 3.6 %copy-start = (bf16[256,512]{1,0:T(8,128)(2,1)S(1)}, bf16[256,512]{1,0:T(8,128)(2,1)}, u32[]{:S(2)}) copy-start(bf16[256,512]{1,0:T(8,128)(2,1)} %get-tuple-element.18) | copy-start | bytes 786436
  87.0 4.3 %copy-start.2 = (f32[1,256]{1,0:T(1,128)S(1)}, f32[1,256]{1,0:T(1,128)}, u32[]{:S(2)}) copy-start(f32[1,256]{1,0:T(1,128)} %get-tuple-element.19) | copy-start | bytes 3076
  87.0 4.9 %copy-start.1 = (f32[1,256]{1,0:T(1,128)S(1)}, f32[1,256]{1,0:T(1,128)}, u32[]{:S(2)}) copy-start(f32[1,256]{1,0:T(1,128)} %get-tuple-element.20) | copy-start | bytes 3076

commit v4 on v3

--- a/solution.py
+++ b/solution.py
@@ -1,5 +1,6 @@
 import jax
 import jax.numpy as jnp
+import numpy as np
 from jax import lax
 from jax.experimental import pallas as pl
 from jax.experimental.pallas import tpu as pltpu
@@ -308,10 +309,10 @@
             "dp": lax.div(z_other, z_lo_size) * X_SIZE + x_pos,
         }
 
-    stages = ((LOW, peer_a, low), (X_SIZE, peer_b, x_pos), (z_size, peer_c, z_pos))
+    stages = ((z_size, peer_c, z_pos), (LOW, peer_a, low), (X_SIZE, peer_b, x_pos))
     barrier = pltpu.get_barrier_semaphore()
     greeted = 0
-    for size, peer, _ in reversed(stages):
+    for size, peer, _ in stages:
         for k in range(1, size):
             pl.semaphore_signal(barrier, inc=1, device_id=peer(k), device_id_type=MESH)
             greeted += 1
@@ -343,8 +344,8 @@
 
     sources = (x_ref, part_b, part_c)
     results = (part_b, part_c, x_ref)
-    slot_refs = (slots_a, slots_b, slots_c)
-    bases = (0, LOW - 1, LOW + X_SIZE - 2)
+    slot_refs = (slots_c, slots_a, slots_b)
+    bases = (0, z_size - 1, z_size + LOW - 2)
 
     def gain_copies(stage):
         size, peer, _ = stages[stage]
@@ -520,19 +521,39 @@
     )(*args)
 
 
+def hand_out_kernel(*refs):
+    half = len(refs) // 2
+    for source, target in zip(refs[:half], refs[half:]):
+        target[...] = source[...]
+
+
+def hand_out(*results):
+    return pl.pallas_call(
+        hand_out_kernel,
+        out_shape=tuple(jax.ShapeDtypeStruct(r.shape, r.dtype) for r in results),
+        in_specs=[VMEM_SPEC] * len(results),
+        out_specs=(VMEM_SPEC,) * len(results),
+        name="hand_out",
+    )(*results)
+
+
 def local(seq_size, dp_size, q_raw, k_raw, values, grad_out, q_gain, k_gain):
     q_local, k_local, v_local, do_local = q_raw[0], k_raw[0], values[0], grad_out[0]
     rows = k_local.shape[0]
     head_size = q_gain.shape[0]
     positions = lax.axis_index("seq") * rows + jnp.arange(rows, dtype=jnp.int32)
     cosine, sine = rope_tables(positions, head_size)
-    back = jnp.maximum(4 - jnp.arange(8, dtype=jnp.int32), 0) * (2 * rows)
-    turn = jnp.concatenate(rope_tables(back, head_size), axis=-1)
+    back = np.maximum(4 - np.arange(8), 0)[:, None] * (2.0 * rows)
+    angles = back * ROPE_BASE ** (-2.0 * np.arange(head_size // 2) / head_size)
+    turn = jnp.asarray(np.concatenate([np.cos(angles), np.sin(angles)], -1), jnp.float32)
     q_gain, k_gain = q_gain[None], k_gain[None]
     q_rot, keys, vals = halo(seq_size, q_local, k_local, v_local, q_gain, k_gain, cosine, sine)
     grad_q, grad_k, grad_v, grad_q_gain, grad_k_gain = backward(
         seq_size, dp_size, q_rot, keys, vals, do_local, q_local, k_local, q_gain, k_gain,
         cosine, sine, turn,
+    )
+    grad_q, grad_k, grad_v, grad_q_gain, grad_k_gain = hand_out(
+        grad_q, grad_k, grad_v, grad_q_gain, grad_k_gain
     )
     return (grad_q[None], grad_k[None], grad_v[None], grad_q_gain[0], grad_k_gain[0])
 

time: 92.6 us -> 87.5 us (0.945)
  local copies, waits for them, and re-layouts: 5.42 us -> 0 us
    unnamed x11 -> x0, local copies, waits for them, and re-layouts: 5.42 us -> none
    pallas_call x0 -> x1, Pallas kernels: none -> 2.18 us  [hand_out(): pl.pallas_call(hand_out_kernel, out_shape=tuple((jax.ShapeDtypeStruct(r.s...]
    pallas_call x1, Pallas kernels: 55.3 us -> 53.6 us  [backward(): pl.pallas_call(lambda *refs: backward_kernel(seq_size, dp_size, *refs), o...]
where the time goes in v4:
time: 87.5 us; the launch traced here: 86.7 us
  Pallas kernels  84.8 us (97%)
  other arithmetic  1.25 us (1%)
    pallas_call x1, Pallas kernels, backward(): pl.pallas_call(lambda *refs: backward_kernel(seq_size, dp_size, *refs), o...  53.6 us
    pallas_call x1, Pallas kernels, halo(): pl.pallas_call(lambda *refs: halo_kernel(seq_size, *refs), out_shape=(jax...  29 us
    pallas_call x1, Pallas kernels, hand_out(): pl.pallas_call(hand_out_kernel, out_shape=tuple((jax.ShapeDtypeStruct(r.s...  2.18 us

profile of v4, /device:TPU:25, one launch (start us, length us, event | category | flops | bytes accessed | tf_op | source)
XLA Modules:
  0.0 86.7 jit_solution(1421118394327164507)
XLA Ops:
  0.7 1.2 %multiply_sine_fusion = (f32[256,128]{1,0:T(8,128)}, f32[256,128]{1,0:T(8,128)}) fusion(f32[128]{0:T(128)S(1)} %multiply_power_fusion, f32[256]{0:T(256)S(1)} %add_convert_fusion), kind=kLoop, calls=%fused_computation | loop fusion | flops 32768 | bytes 263680 | tf_op jit(solution)/shard_map/sin | solution.py:25
  1.9 29.0 %halo.1 = (bf16[256,1024]{1,0:T(8,128)(2,1)}, bf16[5,256,512]{2,1,0:T(8,128)(2,1)}, bf16[5,256,512]{2,1,0:T(8,128)(2,1)}) custom-call(bf16[256,1024]{1,0:T(8,128)(2,1)} %bitcast.11, bf16[256,512]{1,0:T(8,128)(2,1)} %bitcast.13, bf16[256,512]{1,0:T(8,128)(2,1)} %bitcast.16, f32[1,256]{1,0:T(1,128)} %bitcast.17, f32[1,256]{1,0:T(1,128)} %bitcast.19, ...), custom_call_target="tpu_custom_call" | custom-call | tf_op jit(solution)/shard_map/halo/pallas_call | solution.py:464
  30.9 53.6 %backward.1 = (bf16[256,1024]{1,0:T(8,128)(2,1)}, bf16[256,512]{1,0:T(8,128)(2,1)}, bf16[256,512]{1,0:T(8,128)(2,1)}, f32[1,256]{1,0:T(1,128)}, f32[1,256]{1,0:T(1,128)}) custom-call(bf16[256,1024]{1,0:T(8,128)(2,1)} %get-tuple-element.18.refs_0_, bf16[5,256,512]{2,1,0:T(8,128)(2,1)} %get-tuple-element.19.refs_1_, ...), custom_call_target="tpu_custom_call" | custom-call | tf_op jit(solution)/shard_map/backward/pallas_call | solution.py:490
  84.5 2.2 %hand_out.1 = (bf16[256,1024]{1,0:T(8,128)(2,1)}, bf16[256,512]{1,0:T(8,128)(2,1)}, bf16[256,512]{1,0:T(8,128)(2,1)}, f32[1,256]{1,0:T(1,128)}, f32[1,256]{1,0:T(1,128)}) custom-call(bf16[256,1024]{1,0:T(8,128)(2,1)} %get-tuple-element.21.refs_0_, bf16[256,512]{1,0:T(8,128)(2,1)} %get-tuple-element.22.refs_1_, bf16[256,512]{1,0:T(8,128)(2,1)} %get-tuple-element.23.refs_2_, ...), custom_call_target="tpu_custom_call" | custom-call | tf_op jit(solution)/shard_map/hand_out/pallas_call | solution.py:531
  (2 shorter events, 0.0 us)

commit v5 on v4

--- a/solution.py
+++ b/solution.py
@@ -309,7 +309,7 @@
             "dp": lax.div(z_other, z_lo_size) * X_SIZE + x_pos,
         }
 
-    stages = ((z_size, peer_c, z_pos), (LOW, peer_a, low), (X_SIZE, peer_b, x_pos))
+    stages = ((z_size, peer_c, z_pos), (X_SIZE, peer_b, x_pos), (LOW, peer_a, low))
     barrier = pltpu.get_barrier_semaphore()
     greeted = 0
     for size, peer, _ in stages:
@@ -344,8 +344,8 @@
 
     sources = (x_ref, part_b, part_c)
     results = (part_b, part_c, x_ref)
-    slot_refs = (slots_c, slots_a, slots_b)
-    bases = (0, z_size - 1, z_size + LOW - 2)
+    slot_refs = (slots_c, slots_b, slots_a)
+    bases = (0, z_size - 1, z_size + X_SIZE - 2)
 
     def gain_copies(stage):
         size, peer, _ = stages[stage]
@@ -426,8 +426,9 @@
         def _():
             hop(which, 1).start()
 
-        gain_end(which)
-        gain_start(which + 1)
+    for stage in range(2):
+        gain_end(stage)
+        gain_start(stage + 1)
 
     for which in range(2):
 

time: 87.5 us -> 83.2 us (0.951)
  Pallas kernels: 84.8 us -> 81.1 us
    pallas_call x1, Pallas kernels: 53.6 us -> 49.9 us  [backward(): pl.pallas_call(lambda *refs: backward_kernel(seq_size, dp_size, *refs), o...]
where the time goes in v5:
time: 83.2 us; the launch traced here: 83 us
  Pallas kernels  81.1 us (97%)
  other arithmetic  1.25 us (2%)
    pallas_call x1, Pallas kernels, backward(): pl.pallas_call(lambda *refs: backward_kernel(seq_size, dp_size, *refs), o...  49.9 us
    pallas_call x1, Pallas kernels, halo(): pl.pallas_call(lambda *refs: halo_kernel(seq_size, *refs), out_shape=(jax...  29 us
    pallas_call x1, Pallas kernels, hand_out(): pl.pallas_call(hand_out_kernel, out_shape=tuple((jax.ShapeDtypeStruct(r.s...  2.18 us

profile of v5, /device:TPU:25, one launch (start us, length us, event | category | flops | bytes accessed | tf_op | source)
XLA Modules:
  0.0 83.0 jit_solution(4508780319048314340)
XLA Ops:
  0.7 1.2 %multiply_sine_fusion = (f32[256,128]{1,0:T(8,128)}, f32[256,128]{1,0:T(8,128)}) fusion(f32[128]{0:T(128)S(1)} %multiply_power_fusion, f32[256]{0:T(256)S(1)} %add_convert_fusion), kind=kLoop, calls=%fused_computation | loop fusion | flops 32768 | bytes 263680 | tf_op jit(solution)/shard_map/sin | solution.py:25
  1.9 29.0 %halo.1 = (bf16[256,1024]{1,0:T(8,128)(2,1)}, bf16[5,256,512]{2,1,0:T(8,128)(2,1)}, bf16[5,256,512]{2,1,0:T(8,128)(2,1)}) custom-call(bf16[256,1024]{1,0:T(8,128)(2,1)} %bitcast.11, bf16[256,512]{1,0:T(8,128)(2,1)} %bitcast.13, bf16[256,512]{1,0:T(8,128)(2,1)} %bitcast.16, f32[1,256]{1,0:T(1,128)} %bitcast.17, f32[1,256]{1,0:T(1,128)} %bitcast.19, ...), custom_call_target="tpu_custom_call" | custom-call | tf_op jit(solution)/shard_map/halo/pallas_call | solution.py:465
  30.9 49.9 %backward.1 = (bf16[256,1024]{1,0:T(8,128)(2,1)}, bf16[256,512]{1,0:T(8,128)(2,1)}, bf16[256,512]{1,0:T(8,128)(2,1)}, f32[1,256]{1,0:T(1,128)}, f32[1,256]{1,0:T(1,128)}) custom-call(bf16[256,1024]{1,0:T(8,128)(2,1)} %get-tuple-element.18.refs_0_, bf16[5,256,512]{2,1,0:T(8,128)(2,1)} %get-tuple-element.19.refs_1_, ...), custom_call_target="tpu_custom_call" | custom-call | tf_op jit(solution)/shard_map/backward/pallas_call | solution.py:491
  80.8 2.2 %hand_out.1 = (bf16[256,1024]{1,0:T(8,128)(2,1)}, bf16[256,512]{1,0:T(8,128)(2,1)}, bf16[256,512]{1,0:T(8,128)(2,1)}, f32[1,256]{1,0:T(1,128)}, f32[1,256]{1,0:T(1,128)}) custom-call(bf16[256,1024]{1,0:T(8,128)(2,1)} %get-tuple-element.21.refs_0_, bf16[256,512]{1,0:T(8,128)(2,1)} %get-tuple-element.22.refs_1_, bf16[256,512]{1,0:T(8,128)(2,1)} %get-tuple-element.23.refs_2_, ...), custom_call_target="tpu_custom_call" | custom-call | tf_op jit(solution)/shard_map/hand_out/pallas_call | solution.py:532
  (2 shorter events, 0.0 us)
